TPU v7x, 128 devices: a whole 4x4x4 slice. The times are simulated.
128 devices in a mesh: row: 8 (over z, core), col: 16 (over y, x).
Axes of the slice: x: 4, y: 4, z: 4, core: 2. Of those that a mesh axis runs over, the one named last changes fastest.
Arguments:
- snapshots: bfloat16 [4096, 32768], P('row', 'col'), may hold values from -14 to 14
- neighbours: int32 [4096, 128], P('row'), may hold values from 0 to 4095, all different within a row
- start_basis: float32 [32, 4096], replicated, may hold values from -6 to 6
Outputs:
- basis: float32 [32, 4096], P(None, 'row')
- rayleigh: float32 [32, 32], replicated
Inputs may be any that keep to these rules, and one draw needn't show every extreme that they name: `neighbours`: each row names 128 different snapshots.
All inputs are finite; a program needn't handle non-finite values.
Results may differ from a plain program's by a relative error of at most 0.00145.
Values may be sent and summed in bfloat16 or wider, within the bound.
No kernel may reach another device: no remote copies, remote signals or barrier semaphores. Data moves between devices by JAX's collectives and lax.ppermute only.
A program may use at most 128 MiB of HBM per device.

v0:
```python
import functools

import jax
import jax.numpy as jnp
from jax import lax
from jax.experimental import pallas as pl
from jax.experimental.pallas import tpu as pltpu
from jax.sharding import PartitionSpec as P

SNAPS = 4096
FEATURES = 32768
LAGS = 64
BLOCK = 512
MB = 32
PAD = SNAPS + 128
GROUP = 8
NT = (((1,), (1,)), ((), ()))
F32 = jnp.float32
BF16 = jnp.bfloat16


def row_perm(step, flip):
    return [(2 * z + c, 2 * ((z + step) % 4) + (c ^ flip)) for z in range(4) for c in range(2)]


def col_perm(dy, dx):
    return [(4 * y + x, 4 * ((y + dy) % 4) + (x + dx) % 4) for y in range(4) for x in range(4)]


def squares(x):
    f = x.astype(F32)
    q = f * f
    hi = q.astype(BF16)
    return hi, (q - hi.astype(F32)).astype(BF16)


def pick_kernel(where_ref, p0, p1, p2, p3, q0, q1, q2, q3, nb_ref, out_ref, x_ref, nj_ref, nt_ref, g_ref, perm_ref, ring_ref, s_ref, carry_ref, acc_ref, sem):
    step = pl.program_id(0)
    z = where_ref[0]
    par = where_ref[1]
    lane = lax.broadcasted_iota(jnp.int32, (8, 128), 1)
    m0 = (step - 2) * MB

    def block_rows(d, parity):
        b = 2 * lax.rem(z + d, 4) + parity
        return pl.ds(pl.multiple_of(b * BLOCK, BLOCK), BLOCK)

    @pl.when(step == 0)
    def _():
        copies = []
        for d, (p, q) in enumerate(((p0, q0), (p1, q1), (p2, q2), (p3, q3))):
            copies.append(pltpu.make_async_copy(p, x_ref.at[block_rows(d, par)], sem.at[d]))
            copies.append(pltpu.make_async_copy(q, x_ref.at[block_rows(d, 1 - par)], sem.at[4 + d]))
        for c in copies:
            c.start()
        carry_ref[...] = jnp.zeros_like(carry_ref)
        ri = lax.broadcasted_iota(jnp.int32, (256, 256), 0)
        ci = lax.broadcasted_iota(jnp.int32, (256, 256), 1)
        perm_ref[...] = jnp.where(ci == lax.rem(ri, 8) * MB + lax.div(ri, 8), 1.0, 0.0).astype(BF16)
        for c in copies:
            c.wait()
        halves = jnp.full((8, BLOCK), 0.5, BF16)
        for b in range(16):
            hi, lo = squares(x_ref[b * 256 : (b + 1) * 256, :])
            nj_ref[:, b * 256 : (b + 1) * 256] = lax.dot_general(
                halves, hi, NT, preferred_element_type=F32
            ) + lax.dot_general(halves, lo, NT, preferred_element_type=F32)

    rows = []
    for a in range(8):
        t = 1024 * lax.rem(z + a // 2, 4) + BLOCK * par + 256 * (a % 2) + m0
        rows.append(x_ref[pl.ds(pl.multiple_of(jnp.maximum(t, 0), MB), MB), :])
    lhs = jnp.dot(perm_ref[...], jnp.concatenate(rows, 0), preferred_element_type=F32).astype(BF16)
    halves = jnp.full((BLOCK, 128), 0.5, BF16)
    hi, lo = squares(lhs)
    nt_ref[...] = jnp.dot(hi, halves, preferred_element_type=F32) + jnp.dot(lo, halves, preferred_element_type=F32)
    for jb in range(8):
        r = lax.dot_general(lhs, x_ref[jb * BLOCK : (jb + 1) * BLOCK, :], NT, preferred_element_type=F32)
        for k in range(4):
            g_ref[jb * 4 + k] = r[:, k * 128 : (k + 1) * 128]

    def window_sums(base, halo, i):
        shifts, masks, nts, valids = [], [], [], []
        ring = ring_ref.at[lax.rem(step, LAGS // MB) * (MB // GROUP) + i]
        sums = s_ref.at[i]
        here = g_ref.at[:, pl.ds(pl.multiple_of(i * (8 * GROUP), 8 * GROUP), 8 * GROUP), :]
        nt_here = nt_ref.at[pl.ds(pl.multiple_of(i * (8 * GROUP), 8 * GROUP), 8 * GROUP), :]
        for u in range(GROUP):
            m = m0 + i * GROUP + u
            shifts.append(lax.rem(256 - lax.rem(m + 128, 128), 128))
            masks.append(lane < 128 - lax.rem(m + 128, 128))
            nts.append(nt_here[u * 8 : u * 8 + 8, :])
            if halo:
                a = lax.broadcasted_iota(jnp.int32, (8, 128), 0)
                first_t = 1024 * lax.rem(z + lax.div(a, 2), 4) + BLOCK * par + 256 * lax.rem(a, 2)
                valids.append(first_t + m >= 0)
        cache = [{} for _ in range(GROUP)]

        def term(u, c):
            v = (nj_ref[:, c * 128 : (c + 1) * 128] + nts[u]) - here[c, u * 8 : u * 8 + 8, :]
            return jnp.where(valids[u], v, 0.0) if halo else v

        def rolled(u, c):
            if c == 32:
                return jnp.zeros((8, 128), F32)
            low = c - c % 2
            if low not in cache[u]:
                both = jnp.concatenate([term(u, low), term(u, low + 1)], 0).astype(BF16)
                both = pltpu.roll(both, shifts[u], 1).astype(F32)
                cache[u][low], cache[u][low + 1] = both[:8], both[8:]
            return cache[u][c]

        for cd in range(33):
            col = slice(cd * 128, (cd + 1) * 128)
            s = carry_ref[:, col]
            for u in range(GROUP):
                row = slice(u * 8, u * 8 + 8)
                d = jnp.where(masks[u], rolled(u, (cd + base) % 33), rolled(u, (cd + base + 1) % 33))
                if halo:
                    s = s + d
                else:
                    s = s + (d - ring[row, col])
                    sums[row, col] = s
                ring[row, col] = d
            carry_ref[:, col] = s

    def look_up(i, u):
        mi = i * GROUP + u
        p = nb_ref[mi] - (m0 + mi)
        p = jnp.where(p < 0, p + PAD, p)
        hi = lax.shift_right_logical(p, 7)
        lo = p & 127
        sums = s_ref.at[i]
        accs = []
        for part in range(3):
            acc = jnp.zeros((8, 128), F32)
            for cd in range(part * 11, part * 11 + 11):
                g = jnp.take_along_axis(sums[u * 8 : u * 8 + 8, cd * 128 : (cd + 1) * 128], lo, axis=1, mode="promise_in_bounds")
                acc = jnp.where(hi == cd, g, acc)
            accs.append(acc)
        acc_ref[pl.ds(pl.multiple_of(mi * 8, 8), 8), :] = jnp.where(hi < 11, accs[0], jnp.where(hi < 22, accs[1], accs[2]))

    def windows(base, halo):
        def body(i, carry):
            window_sums(base, halo, i)
            return carry

        lax.fori_loop(0, MB // GROUP, body, 0)

    pl.when(step < 2)(functools.partial(windows, -1, True))
    pl.when((step >= 2) & (step < 6))(functools.partial(windows, 0, False))
    pl.when(step >= 6)(functools.partial(windows, 1, False))

    @pl.when(step >= 2)
    def _():
        def body(i, carry):
            for u in range(GROUP):
                look_up(i, u)
            return carry

        lax.fori_loop(0, MB // GROUP, body, 0)
        for a in range(8):
            for k in range(MB // 8):
                out_ref[a, k * 8 : (k + 1) * 8, :] = acc_ref[pl.ds(k * 64 + a, 8, stride=8), :]


def pick(where, own, other, nb):
    anywhere = pl.BlockSpec(memory_space=pl.ANY)
    return pl.pallas_call(
        pick_kernel,
        grid_spec=pltpu.PrefetchScalarGridSpec(
            num_scalar_prefetch=1,
            grid=(10,),
            in_specs=[anywhere] * 8
            + [
                pl.BlockSpec((MB, 8, 128), lambda i, w: (jnp.maximum(i - 2, 0), 0, 0)),
            ],
            out_specs=pl.BlockSpec((8, MB, 128), lambda i, w: (0, jnp.maximum(i - 2, 0), 0)),
            scratch_shapes=[
                pltpu.VMEM((SNAPS, BLOCK), BF16),
                pltpu.VMEM((8, SNAPS), F32),
                pltpu.VMEM((256, 128), F32),
                pltpu.VMEM((32, 256, 128), F32),
                pltpu.VMEM((256, 256), BF16),
                pltpu.VMEM((LAGS // GROUP, 8 * GROUP, PAD), F32),
                pltpu.VMEM((MB // GROUP, 8 * GROUP, PAD), F32),
                pltpu.VMEM((8, PAD), F32),
                pltpu.VMEM((256, 128), F32),
                pltpu.SemaphoreType.DMA((8,)),
            ],
        ),
        out_shape=jax.ShapeDtypeStruct((8, 256, 128), F32),
        compiler_params=pltpu.CompilerParams(vmem_limit_bytes=40 * 1024 * 1024),
        name="pick",
    )(where, *own, *other, nb)


def slot_map_kernel(nb_ref, out_ref):
    sub32 = lax.broadcasted_iota(jnp.int32, (32, 128), 0)
    sub128 = lax.broadcasted_iota(jnp.int32, (128, 128), 0)
    number = lax.broadcasted_iota(jnp.int32, (32, 128), 1).astype(F32) + 1.0

    def body(t, carry):
        nb = nb_ref[pl.ds(t, 1), :]
        hi = jnp.broadcast_to(lax.shift_right_logical(nb, 7), (32, 128))
        lo = jnp.broadcast_to(nb & 127, (128, 128))
        left = jnp.where(sub32 == hi, number, 0.0).astype(BF16)
        right = jnp.where(sub128 == lo, 1.0, 0.0).astype(BF16)
        out_ref[t] = lax.dot_general(left, right, NT, preferred_element_type=F32).astype(jnp.int32)
        return carry

    lax.fori_loop(0, 64, body, 0, unroll=8)


def slot_map(nb):
    return pl.pallas_call(
        slot_map_kernel,
        grid=(8,),
        in_specs=[pl.BlockSpec((64, 128), lambda i: (i, 0))],
        out_specs=pl.BlockSpec((64, 32, 128), lambda i: (i, 0, 0)),
        out_shape=jax.ShapeDtypeStruct((BLOCK, 32, 128), jnp.int32),
        cost_estimate=pl.CostEstimate(flops=1 << 20, bytes_accessed=1 << 20, transcendentals=0),
        name="slot_map",
    )(nb)


def split3(x):
    hi = x.astype(BF16)
    rest = x - hi.astype(F32)
    mid = rest.astype(BF16)
    return hi, mid, (rest - mid.astype(F32)).astype(BF16)


def times_transposed(parts, hi, lo):
    r = lax.dot_general(parts, hi, NT, preferred_element_type=F32)
    q = lax.dot_general(parts[:64], lo, NT, preferred_element_type=F32)
    return ((r[64:] + q[32:]) + (r[32:64] + q[:32])) + r[:32]


def operator_kernel(sum_ref, map_ref, b_ref, hi_ref, lo_ref, out_ref):
    kernel = 1.0 / (1.0 + sum_ref[...] * (2.0 / (LAGS * FEATURES)))
    mass = jnp.sum(kernel, axis=1, keepdims=True)
    markov = kernel / mass
    for g in range(8):
        w = [markov[g * 16 + h * 8 : g * 16 + h * 8 + 8, :] for h in range(2)]
        for c in range(32):
            col = slice(c * 128, (c + 1) * 128)
            values = []
            for h in range(2):
                at = map_ref[g * 16 + h * 8 : g * 16 + h * 8 + 8, col]
                value = jnp.take_along_axis(w[h], (at - 1) & 127, axis=1, mode="promise_in_bounds")
                values.append(jnp.where(at > 0, value, 0.0))
            v = jnp.concatenate(values, 0)
            hi = v.astype(BF16)
            hi_ref[g * 16 : (g + 1) * 16, col] = hi
            lo_ref[g * 16 : (g + 1) * 16, col] = (v - hi.astype(F32)).astype(BF16)
    out_ref[...] = times_transposed(jnp.concatenate(split3(b_ref[...]), 0), hi_ref[...], lo_ref[...])


def operator(total, slots, start):
    return pl.pallas_call(
        operator_kernel,
        grid=(4,),
        in_specs=[
            pl.BlockSpec((128, 128), lambda i: (i, 0)),
            pl.BlockSpec((128, SNAPS), lambda i: (i, 0)),
            pl.BlockSpec((32, SNAPS), lambda i: (0, 0)),
        ],
        out_specs=[
            pl.BlockSpec((128, SNAPS), lambda i: (i, 0)),
            pl.BlockSpec((128, SNAPS), lambda i: (i, 0)),
            pl.BlockSpec((32, 128), lambda i: (0, i)),
        ],
        out_shape=[
            jax.ShapeDtypeStruct((BLOCK, SNAPS), BF16),
            jax.ShapeDtypeStruct((BLOCK, SNAPS), BF16),
            jax.ShapeDtypeStruct((32, BLOCK), F32),
        ],
        name="operator",
    )(total, slots, start)


def apply_kernel(hi_ref, lo_ref, *refs):
    pieces, out_ref = refs[:-1], refs[-1]
    halves = len(pieces)
    full = jnp.concatenate([p[:, : SNAPS // halves] for p in pieces], 1)
    out_ref[...] = times_transposed(jnp.concatenate(split3(full), 0), hi_ref[...], lo_ref[...])


def apply_rows(hi, lo, pieces):
    whole = pl.BlockSpec((32, pieces[0].shape[1]), lambda i: (0, 0))
    return pl.pallas_call(
        apply_kernel,
        grid=(2,),
        in_specs=[pl.BlockSpec((256, SNAPS), lambda i: (i, 0))] * 2 + [whole] * len(pieces),
        out_specs=pl.BlockSpec((32, 256), lambda i: (0, i)),
        out_shape=jax.ShapeDtypeStruct((32, BLOCK), F32),
        name="apply",
    )(hi, lo, *pieces)


def sum_four(v, axis, perms):
    r1, r2, r3 = [lax.ppermute(v, axis, p) for p in perms]
    v, r1, r2, r3 = [a.astype(F32) for a in (v, r1, r2, r3)]
    return (v + r2) + (r1 + r3)


def mul(a, b, dims=(((1,), (0,)), ((), ()))):
    return lax.dot_general(a, b, dims, precision=lax.Precision.HIGHEST, preferred_element_type=F32)


def shards(snapshots, neighbours, start_basis):
    row_at = lax.axis_index("row")
    z = row_at // 2
    par = row_at % 2
    z_send = [row_perm(d, 0) for d in (1, 2, 3)]
    core_swap = row_perm(0, 1)
    width = snapshots.shape[1] // 4

    def piece(d):
        at = ((z + d) % 4) * width
        return lax.dynamic_slice_in_dim(snapshots, at, width, 1)

    nb16 = neighbours.astype(jnp.int16)
    nb_from = [neighbours] + [None] * 3
    for d in (1, 2, 3):
        nb_from[4 - d] = lax.ppermute(nb16, "row", z_send[d - 1])
    own = [piece(0)] + [None] * 3
    for d in (2, 1, 3):
        own[4 - d] = lax.ppermute(piece(d), "row", z_send[d - 1])
    other = [lax.ppermute(a, "row", core_swap) for a in own]
    block = neighbours // BLOCK
    relative = (((block % 2) ^ par) * 4 + ((block // 2 - z) % 4)) * BLOCK + neighbours % BLOCK
    slots = slot_map(relative)
    order = jnp.arange(8, dtype=jnp.int32)
    order = 2 * ((order % 4 + z) % 4) + ((order // 4) ^ par)
    start = jnp.take(start_basis.reshape(32, 8, BLOCK), order, axis=1).reshape(32, SNAPS)

    where = jnp.stack([z, par]).astype(jnp.int32)
    nb_all = jnp.stack([a.astype(jnp.int32) for a in nb_from]).reshape(8, 256, 128).transpose(1, 0, 2)
    where, slots = lax.optimization_barrier((where, slots))
    chosen = pick(where, own, other, nb_all).reshape(4, BLOCK, 128)

    sent = chosen.astype(BF16)
    r1, r2, r3 = [lax.ppermute(sent[d], "row", z_send[d - 1]) for d in (1, 2, 3)]
    total = (chosen[0] + r2.astype(F32)) + (r1.astype(F32) + r3.astype(F32))
    total = sum_four(total.astype(BF16), "col", [col_perm(0, d) for d in (1, 2, 3)])
    total = sum_four(total, "col", [col_perm(d, 0) for d in (1, 2, 3)])

    def gather_all(v):
        parts = [v] + [None] * 3
        for d in (1, 2, 3):
            parts[4 - d] = lax.ppermute(v, "row", z_send[d - 1])
        gram = (parts[0][:, BLOCK:] + parts[2][:, BLOCK:]) + (parts[1][:, BLOCK:] + parts[3][:, BLOCK:])
        near = jnp.concatenate([p[:, :BLOCK] for p in parts] + [gram], 1)
        far = lax.ppermute(near, "row", core_swap)
        return (near, far), gram + far[:, SNAPS // 2 :]

    hi, lo, image1 = operator(total, slots.reshape(BLOCK, SNAPS), start)
    full1, gram1 = gather_all(jnp.concatenate([image1, mul(image1, image1, NT)], 1))
    image2 = apply_rows(hi, lo, full1)
    full2, gram2 = gather_all(jnp.concatenate([image2, mul(image2, image2, NT)], 1))
    image3 = apply_rows(hi, lo, full2)
    cross = mul(image2, image3, NT)
    cross = sum_four(cross, "row", z_send)
    cross = cross + lax.ppermute(cross, "row", core_swap)

    eye = jnp.eye(32, dtype=F32)
    lower1 = jnp.linalg.cholesky(gram1 / SNAPS)
    inv1 = jax.scipy.linalg.solve_triangular(lower1, eye, lower=True)
    lower2 = jnp.linalg.cholesky(mul(mul(inv1, gram2), inv1, NT) / SNAPS)
    inv = mul(jax.scipy.linalg.solve_triangular(lower2, eye, lower=True), inv1)
    basis = mul(inv, image2)
    rayleigh = mul(mul(inv, cross), inv, NT) / SNAPS
    return basis, rayleigh


def solution(mesh):
    placed = (P("row", "col"), P("row", None), P())
    return jax.shard_map(
        shards, mesh=mesh, in_specs=placed, out_specs=(P(None, "row"), P()), check_vma=False
    )
```

profile of v0, /device:TPU:1, one launch (start us, length us, event | category | flops | bytes accessed | tf_op | source)
XLA Modules:
  0.0 206.0 jit_solution(14923026835516415325)
XLA Ops:
  0.7 2.6 %constant_dynamic-slice_fusion = (bf16[512,512]{1,0:T(8,128)(2,1)S(1)}, bf16[512,512]{1,0:T(8,128)(2,1)}, bf16[512,512]{1,0:T(8,128)(2,1)S(1)}, bf16[512,512]{1,0:T(8,128)(2,1)S(1)}) fusion(bf16[512,2048]{1,0:T(8,128)(2,1)} %param.6, s32[]{:T(128)S(6)} %select_n.146, s32[]{:T(128)S(6)} %select_n.142, s32[]{:T(128)S(6)} %select_n.140, s32[]{:T(128)S(6)} %select_n.144), kind=kLoop, calls=%fused_computation.101 | loop fusion | bytes 4194320 | tf_op jit(solution)/shard_map/dynamic_slice | solution.py:322
  3.4 4.6 %collective-permute-start = (bf16[512,512]{1,0:T(8,128)(2,1)}, bf16[512,512]{1,0:T(8,128)(2,1)S(1)}, u32[]{:S(2)}, u32[]{:S(2)}) collective-permute-start(bf16[512,512]{1,0:T(8,128)(2,1)} %get-tuple-element.25), channel_id=1, source_target_pairs={{0,96},{16,112},{32,0},{48,16},{64,32},{80,48},{96,64},{112,80},{1... | collective-permute-start | bytes 1572872 | tf_op jit(solution)/shard_map/ppermute | solution.py:330
  8.6 1.3 fusion.42
  9.9 1.9 collective-permute-start.9
  11.9 1.2 collective-permute-start.8
  13.2 18.3 %slot_map.1 = s32[512,32,128]{2,1,0:T(8,128)} custom-call(s32[512,128]{1,0:T(8,128)} %get-tuple-element.32.nb_ref), custom_call_target="tpu_custom_call" | custom-call | flops 1048576 | bytes 1048576 | tf_op jit(solution)/shard_map/slot_map/pallas_call | solution.py:216
  31.5 5.9 %collective-permute-done.9 = s16[512,128]{1,0:T(8,128)(2,1)} collective-permute-done((s16[512,128]{1,0:T(8,128)(2,1)S(1)}, s16[512,128]{1,0:T(8,128)(2,1)}, u32[]{:S(2)}, u32[]{:S(2)}) %collective-permute-start.9) | collective-permute-done | bytes 131104 | tf_op jit(solution)/shard_map/ppermute | solution.py:327
  37.5 0.9 bitcast_convert_fusion
  38.7 2.3 %collective-permute-start.3 = (bf16[512,512]{1,0:T(8,128)(2,1)S(1)}, bf16[512,512]{1,0:T(8,128)(2,1)S(1)}, u32[]{:S(2)}, u32[]{:S(2)}) collective-permute-start(bf16[512,512]{1,0:T(8,128)(2,1)S(1)} %get-tuple-element.26.p0), channel_id=1, source_target_pairs={{0,16},{16,0},{32,48},{48,32},{64,80},{80,64},{96,112},{112,96},{1... | collective-permute-start | bytes 1572872 | tf_op jit(solution)/shard_map/ppermute | solution.py:331
  41.6 0.9 bitcast_convert_fusion.1
  44.8 42.3 %pick.1 = f32[8,256,128]{2,1,0:T(8,128)S(1)} custom-call(s32[2]{0:T(128)S(1)} %pad_add_fusion.1.where_ref, bf16[512,512]{1,0:T(8,128)(2,1)S(1)} %get-tuple-element.26.p0, bf16[512,512]{1,0:T(8,128)(2,1)S(1)} %collective-permute-done.p1, bf16[512,512]{1,0:T(8,128)(2,1)S(1)} %collective-permute-done.1.p2, bf16[512,512]{1,0:T(8,128)(2,1)S(1)} %collective-permute-done.2.p3, ...), custom_call_target="tpu_custom_call" | custom-call | tf_op jit(solution)/shard_map/pick/pallas_call | solution.py:169
  87.9 2.3 %collective-permute-start.12 = (bf16[512,128]{1,0:T(8,128)(2,1)S(1)}, bf16[512,128]{1,0:T(8,128)(2,1)S(1)}, u32[]{:S(2)}, u32[]{:S(2)}) collective-permute-start(bf16[512,128]{1,0:T(8,128)(2,1)S(1)} %bitcast.84), channel_id=1, source_target_pairs={{0,96},{16,112},{32,0},{48,16},{64,32},{80,48},{96,64},{112,80},{1... | collective-permute-start | bytes 393224 | tf_op jit(solution)/shard_map/ppermute | solution.py:345
  91.0 2.6 %collective-permute-done.10 = bf16[512,128]{1,0:T(8,128)(2,1)S(1)} collective-permute-done((bf16[512,128]{1,0:T(8,128)(2,1)S(1)}, bf16[512,128]{1,0:T(8,128)(2,1)S(1)}, u32[]{:S(2)}, u32[]{:S(2)}) %collective-permute-start.10) | collective-permute-done | bytes 131104 | tf_op jit(solution)/shard_map/ppermute | solution.py:345
  93.6 3.4 %collective-permute-done.11 = bf16[512,128]{1,0:T(8,128)(2,1)S(1)} collective-permute-done((bf16[512,128]{1,0:T(8,128)(2,1)S(1)}, bf16[512,128]{1,0:T(8,128)(2,1)S(1)}, u32[]{:S(2)}, u32[]{:S(2)}) %collective-permute-start.11) | collective-permute-done | bytes 131104 | tf_op jit(solution)/shard_map/ppermute | solution.py:345
  97.0 2.8 %collective-permute-start.13 = (bf16[512,128]{1,0:T(8,128)(2,1)S(1)}, bf16[512,128]{1,0:T(8,128)(2,1)S(1)}, u32[]{:S(2)}, u32[]{:S(2)}) collective-permute-start(bf16[512,128]{1,0:T(8,128)(2,1)S(1)} %fusion.8), channel_id=1, source_target_pairs={{0,2},{1,3},{2,0},{3,1},{4,6},{5,7},{6,4},{7,5},{8,10},{9,11},{10,... | collective-permute-start | bytes 393224 | tf_op jit(solution)/shard_map/ppermute | solution.py:303
  100.2 2.4 %collective-permute-start.15 = (bf16[512,128]{1,0:T(8,128)(2,1)S(1)}, bf16[512,128]{1,0:T(8,128)(2,1)S(1)}, u32[]{:S(2)}, u32[]{:S(2)}) collective-permute-start(bf16[512,128]{1,0:T(8,128)(2,1)S(1)} %fusion.8), channel_id=1, source_target_pairs={{0,3},{1,0},{2,1},{3,2},{4,7},{5,4},{6,5},{7,6},{8,11},{9,8},{10,9... | collective-permute-start | bytes 393224 | tf_op jit(solution)/shard_map/ppermute | solution.py:303
  103.2 3.4 %collective-permute-done.14 = bf16[512,128]{1,0:T(8,128)(2,1)S(1)} collective-permute-done((bf16[512,128]{1,0:T(8,128)(2,1)S(1)}, bf16[512,128]{1,0:T(8,128)(2,1)S(1)}, u32[]{:S(2)}, u32[]{:S(2)}) %collective-permute-start.14) | collective-permute-done | bytes 131104 | tf_op jit(solution)/shard_map/ppermute | solution.py:303
  106.6 3.0 %collective-permute-start.16 = (f32[512,128]{1,0:T(8,128)S(1)}, f32[512,128]{1,0:T(8,128)S(1)}, u32[]{:S(2)}, u32[]{:S(2)}) collective-permute-start(f32[512,128]{1,0:T(8,128)S(1)} %add_add_fusion.1), channel_id=1, source_target_pairs={{0,8},{1,9},{2,10},{3,11},{4,12},{5,13},{6,14},{7,15},{8,0},{9,1},... | collective-permute-start | bytes 786440 | tf_op jit(solution)/shard_map/ppermute | solution.py:303
  110.1 2.3 %collective-permute-start.18 = (f32[512,128]{1,0:T(8,128)S(1)}, f32[512,128]{1,0:T(8,128)S(1)}, u32[]{:S(2)}, u32[]{:S(2)}) collective-permute-start(f32[512,128]{1,0:T(8,128)S(1)} %add_add_fusion.1), channel_id=1, source_target_pairs={{0,12},{1,13},{2,14},{3,15},{4,0},{5,1},{6,2},{7,3},{8,4},{9,5},{1... | collective-permute-start | bytes 786440 | tf_op jit(solution)/shard_map/ppermute | solution.py:303
  112.3 0.9 broadcast_select_fusion.b_ref
  113.2 14.7 %copy.70 = s32[64,8,32,128]{3,1,2,0:T(8,128)} copy(s32[64,8,32,128]{3,2,1,0:T(8,128)} %bitcast.76) | data formatting | bytes 16777216
  128.7 11.7 %operator.1 = (bf16[512,4096]{1,0:T(8,128)(2,1)}, bf16[512,4096]{1,0:T(8,128)(2,1)}, f32[32,512]{1,0:T(8,128)}) custom-call(f32[512,128]{1,0:T(8,128)} %add_add_fusion.sum_ref, s32[512,4096]{1,0:T(8,128)} %bitcast.77, f32[32,4096]{1,0:T(8,128)} %broadcast_select_fusion.b_ref), custom_call_target="tpu_custom_call" | custom-call | tf_op jit(solution)/shard_map/operator/pallas_call | solution.py:261
  140.4 1.1 fusion.43
  141.5 0.8 pad_maximum_fusion
  143.1 2.0 collective-permute-start.19
  145.2 0.8 constant_dynamic-update-slice_fusion.4
  146.1 2.9 %collective-permute-done.20 = f32[32,544]{0,1:T(8,128)S(1)} collective-permute-done((f32[32,544]{0,1:T(8,128)S(1)}, f32[32,544]{0,1:T(8,128)S(1)}, u32[]{:S(2)}, u32[]{:S(2)}) %collective-permute-start.20) | collective-permute-done | bytes 69664 | tf_op jit(solution)/shard_map/ppermute | solution.py:353
  149.1 1.0 collective-permute-done.19
  150.3 8.1 %collective-permute-done.21 = f32[32,544]{0,1:T(8,128)S(1)} collective-permute-done((f32[32,544]{0,1:T(8,128)S(1)}, f32[32,544]{0,1:T(8,128)S(1)}, u32[]{:S(2)}, u32[]{:S(2)}) %collective-permute-start.21) | collective-permute-done | bytes 69664 | tf_op jit(solution)/shard_map/ppermute | solution.py:353
  158.6 1.4 collective-permute-start.22
  160.0 1.2 collective-permute-done.22.refs_1_
  162.0 5.7 %apply.2 = f32[32,512]{1,0:T(8,128)} custom-call(bf16[512,4096]{1,0:T(8,128)(2,1)} %get-tuple-element.12.hi_ref, bf16[512,4096]{1,0:T(8,128)(2,1)} %get-tuple-element.13.lo_ref, f32[32,2080]{1,0:T(8,128)} %copy-done.4, f32[32,2080]{1,0:T(8,128)} %copy-done.6), custom_call_target="tpu_custom_call" | custom-call | tf_op jit(solution)/shard_map/apply/pallas_call | solution.py:292
  167.7 1.1 fusion.44
  168.8 0.8 constant_dynamic-update-slice_fusion.6
  169.6 0.8 pad_maximum_fusion.1
  171.1 1.7 collective-permute-start.23
  173.7 2.9 %cholesky.44 = f32[32,32]{1,0:T(8,128)S(1)} custom-call(f32[32,32]{1,0:T(8,128)S(1)} %fusion.24), custom_call_target="Cholesky" | custom-call | tf_op jit(solution)/shard_map/jit(cholesky)/cholesky | solution.py:369
  177.3 0.9 collective-permute-done.25
  178.2 1.3 collective-permute-start.26
  180.2 2.4 %custom-call.6 = f32[1,32,32]{1,2,0:T(8,128)S(1)} custom-call(f32[1,32,32]{2,1,0:T(8,128)S(1)} %fusion.16), custom_call_target="InvertDiagBlocksLowerTriangular" | custom-call | tf_op jit(solution)/shard_map/jit(_solve_triangular)/triangular_solve | solution.py:370
  183.7 5.7 %apply.3 = f32[32,512]{1,0:T(8,128)} custom-call(bf16[512,4096]{1,0:T(8,128)(2,1)} %get-tuple-element.12.hi_ref, bf16[512,4096]{1,0:T(8,128)(2,1)} %get-tuple-element.13.lo_ref, f32[32,2080]{1,0:T(8,128)} %copy-done.3, f32[32,2080]{1,0:T(8,128)} %copy-done.5), custom_call_target="tpu_custom_call" | custom-call | tf_op jit(solution)/shard_map/apply/pallas_call | solution.py:292
  189.4 1.0 fusion.47
  190.4 1.9 collective-permute-start.27
  192.8 2.1 %collective-permute-start.29 = (f32[32,32]{1,0:T(8,128)S(1)}, f32[32,32]{1,0:T(8,128)S(1)}, u32[]{:S(2)}, u32[]{:S(2)}) collective-permute-start(f32[32,32]{1,0:T(8,128)S(1)} %fusion.47), channel_id=1, source_target_pairs={{0,96},{16,112},{32,0},{48,16},{64,32},{80,48},{96,64},{112,80},{1... | collective-permute-start | bytes 12296 | tf_op jit(solution)/shard_map/ppermute | solution.py:303
  195.0 0.8 fusion.18
  196.1 2.9 %cholesky.55 = f32[32,32]{1,0:T(8,128)S(1)} custom-call(f32[32,32]{1,0:T(8,128)S(1)} %fusion.22), custom_call_target="Cholesky" | custom-call | tf_op jit(solution)/shard_map/jit(cholesky)/cholesky | solution.py:371
  200.3 2.4 %custom-call.7 = f32[1,32,32]{1,2,0:T(8,128)S(1)} custom-call(f32[1,32,32]{2,1,0:T(8,128)S(1)} %fusion.17), custom_call_target="InvertDiagBlocksLowerTriangular" | custom-call | tf_op jit(solution)/shard_map/jit(_solve_triangular)/triangular_solve | solution.py:372
  203.2 0.9 collective-permute-start.30
  (109 shorter events, 17.9 us)
Async XLA Ops:
  0.6 8.0 %copy-start.1 = (s32[512,128]{1,0:T(8,128)S(1)}, s32[512,128]{1,0:T(8,128)}, u32[]{:S(2)}) copy-start(s32[512,128]{1,0:T(8,128)} %param.7) | copy-start | bytes 786436
  3.4 37.6 %collective-permute-start = (bf16[512,512]{1,0:T(8,128)(2,1)}, bf16[512,512]{1,0:T(8,128)(2,1)S(1)}, u32[]{:S(2)}, u32[]{:S(2)}) collective-permute-start(bf16[512,512]{1,0:T(8,128)(2,1)} %get-tuple-element.25), channel_id=1, source_target_pairs={{0,96},{16,112},{32,0},{48,16},{64,32},{80,48},{96,64},{112,80},{1... | collective-permute-start | bytes 1572872 | tf_op jit(solution)/shard_map/ppermute | solution.py:330
  7.9 33.1 %collective-permute-start.1 = (bf16[512,512]{1,0:T(8,128)(2,1)S(1)}, bf16[512,512]{1,0:T(8,128)(2,1)S(1)}, u32[]{:S(2)}, u32[]{:S(2)}) collective-permute-start(bf16[512,512]{1,0:T(8,128)(2,1)S(1)} %get-tuple-element.27), channel_id=1, source_target_pairs={{0,64},{16,80},{32,96},{48,112},{64,0},{80,16},{96,32},{112,48},{1... | collective-permute-start | bytes 1572872 | tf_op jit(solution)/shard_map/ppermute | solution.py:330
  7.9 33.5 %collective-permute-start.2 = (bf16[512,512]{1,0:T(8,128)(2,1)S(1)}, bf16[512,512]{1,0:T(8,128)(2,1)S(1)}, u32[]{:S(2)}, u32[]{:S(2)}) collective-permute-start(bf16[512,512]{1,0:T(8,128)(2,1)S(1)} %get-tuple-element.24), channel_id=1, source_target_pairs={{0,32},{16,48},{32,64},{48,80},{64,96},{80,112},{96,0},{112,16},{1... | collective-permute-start | bytes 1572872 | tf_op jit(solution)/shard_map/ppermute | solution.py:330
  9.9 27.5 %collective-permute-start.9 = (s16[512,128]{1,0:T(8,128)(2,1)S(1)}, s16[512,128]{1,0:T(8,128)(2,1)}, u32[]{:S(2)}, u32[]{:S(2)}) collective-permute-start(s16[512,128]{1,0:T(8,128)(2,1)S(1)} %get-tuple-element.31), channel_id=1, source_target_pairs={{0,32},{16,48},{32,64},{48,80},{64,96},{80,112},{96,0},{112,16},{1... | collective-permute-start | bytes 393224 | tf_op jit(solution)/shard_map/ppermute | solution.py:327
  11.9 26.8 %collective-permute-start.8 = (s16[512,128]{1,0:T(8,128)(2,1)S(1)}, s16[512,128]{1,0:T(8,128)(2,1)}, u32[]{:S(2)}, u32[]{:S(2)}) collective-permute-start(s16[512,128]{1,0:T(8,128)(2,1)S(1)} %get-tuple-element.31), channel_id=1, source_target_pairs={{0,64},{16,80},{32,96},{48,112},{64,0},{80,16},{96,32},{112,48},{1... | collective-permute-start | bytes 393224 | tf_op jit(solution)/shard_map/ppermute | solution.py:327
  37.5 5.1 %collective-permute-start.7 = (s16[512,128]{1,0:T(8,128)(2,1)S(1)}, s16[512,128]{1,0:T(8,128)(2,1)S(1)}, u32[]{:S(2)}, u32[]{:S(2)}) collective-permute-start(s16[512,128]{1,0:T(8,128)(2,1)S(1)} %get-tuple-element.31), channel_id=1, source_target_pairs={{0,96},{16,112},{32,0},{48,16},{64,32},{80,48},{96,64},{112,80},{1... | collective-permute-start | bytes 393224 | tf_op jit(solution)/shard_map/ppermute | solution.py:327
  38.7 4.6 %collective-permute-start.3 = (bf16[512,512]{1,0:T(8,128)(2,1)S(1)}, bf16[512,512]{1,0:T(8,128)(2,1)S(1)}, u32[]{:S(2)}, u32[]{:S(2)}) collective-permute-start(bf16[512,512]{1,0:T(8,128)(2,1)S(1)} %get-tuple-element.26.p0), channel_id=1, source_target_pairs={{0,16},{16,0},{32,48},{48,32},{64,80},{80,64},{96,112},{112,96},{1... | collective-permute-start | bytes 1572872 | tf_op jit(solution)/shard_map/ppermute | solution.py:331
  41.0 2.3 %collective-permute-start.4 = (bf16[512,512]{1,0:T(8,128)(2,1)S(1)}, bf16[512,512]{1,0:T(8,128)(2,1)S(1)}, u32[]{:S(2)}, u32[]{:S(2)}) collective-permute-start(bf16[512,512]{1,0:T(8,128)(2,1)S(1)} %collective-permute-done.p1), channel_id=1, source_target_pairs={{0,16},{16,0},{32,48},{48,32},{64,80},{80,64},{96,112},{112,96},{1... | collective-permute-start | bytes 1572872 | tf_op jit(solution)/shard_map/ppermute | solution.py:331
  41.1 2.9 %collective-permute-start.5 = (bf16[512,512]{1,0:T(8,128)(2,1)S(1)}, bf16[512,512]{1,0:T(8,128)(2,1)S(1)}, u32[]{:S(2)}, u32[]{:S(2)}) collective-permute-start(bf16[512,512]{1,0:T(8,128)(2,1)S(1)} %collective-permute-done.1.p2), channel_id=1, source_target_pairs={{0,16},{16,0},{32,48},{48,32},{64,80},{80,64},{96,112},{112,96},{1... | collective-permute-start | bytes 1572872 | tf_op jit(solution)/shard_map/ppermute | solution.py:331
  41.5 3.3 %collective-permute-start.6 = (bf16[512,512]{1,0:T(8,128)(2,1)S(1)}, bf16[512,512]{1,0:T(8,128)(2,1)S(1)}, u32[]{:S(2)}, u32[]{:S(2)}) collective-permute-start(bf16[512,512]{1,0:T(8,128)(2,1)S(1)} %collective-permute-done.2.p3), channel_id=1, source_target_pairs={{0,16},{16,0},{32,48},{48,32},{64,80},{80,64},{96,112},{112,96},{1... | collective-permute-start | bytes 1572872 | tf_op jit(solution)/shard_map/ppermute | solution.py:331
  44.8 45.5 %copy-start.2 = (f32[32,4096]{1,0:T(8,128)S(1)}, f32[32,4096]{1,0:T(8,128)}, u32[]{:S(2)}) copy-start(f32[32,4096]{1,0:T(8,128)} %param.8) | copy-start | bytes 1572868
  87.2 6.3 %collective-permute-start.10 = (bf16[512,128]{1,0:T(8,128)(2,1)S(1)}, bf16[512,128]{1,0:T(8,128)(2,1)S(1)}, u32[]{:S(2)}, u32[]{:S(2)}) collective-permute-start(bf16[512,128]{1,0:T(8,128)(2,1)S(1)} %bitcast.86), channel_id=1, source_target_pairs={{0,64},{16,80},{32,96},{48,112},{64,0},{80,16},{96,32},{112,48},{1... | collective-permute-start | bytes 393224 | tf_op jit(solution)/shard_map/ppermute | solution.py:345
  87.3 9.6 %collective-permute-start.11 = (bf16[512,128]{1,0:T(8,128)(2,1)S(1)}, bf16[512,128]{1,0:T(8,128)(2,1)S(1)}, u32[]{:S(2)}, u32[]{:S(2)}) collective-permute-start(bf16[512,128]{1,0:T(8,128)(2,1)S(1)} %bitcast.85), channel_id=1, source_target_pairs={{0,32},{16,48},{32,64},{48,80},{64,96},{80,112},{96,0},{112,16},{1... | collective-permute-start | bytes 393224 | tf_op jit(solution)/shard_map/ppermute | solution.py:345
  87.9 9.0 %collective-permute-start.12 = (bf16[512,128]{1,0:T(8,128)(2,1)S(1)}, bf16[512,128]{1,0:T(8,128)(2,1)S(1)}, u32[]{:S(2)}, u32[]{:S(2)}) collective-permute-start(bf16[512,128]{1,0:T(8,128)(2,1)S(1)} %bitcast.84), channel_id=1, source_target_pairs={{0,96},{16,112},{32,0},{48,16},{64,32},{80,48},{96,64},{112,80},{1... | collective-permute-start | bytes 393224 | tf_op jit(solution)/shard_map/ppermute | solution.py:345
  97.0 6.1 %collective-permute-start.13 = (bf16[512,128]{1,0:T(8,128)(2,1)S(1)}, bf16[512,128]{1,0:T(8,128)(2,1)S(1)}, u32[]{:S(2)}, u32[]{:S(2)}) collective-permute-start(bf16[512,128]{1,0:T(8,128)(2,1)S(1)} %fusion.8), channel_id=1, source_target_pairs={{0,2},{1,3},{2,0},{3,1},{4,6},{5,7},{6,4},{7,5},{8,10},{9,11},{10,... | collective-permute-start | bytes 393224 | tf_op jit(solution)/shard_map/ppermute | solution.py:303
  99.9 6.7 %collective-permute-start.14 = (bf16[512,128]{1,0:T(8,128)(2,1)S(1)}, bf16[512,128]{1,0:T(8,128)(2,1)S(1)}, u32[]{:S(2)}, u32[]{:S(2)}) collective-permute-start(bf16[512,128]{1,0:T(8,128)(2,1)S(1)} %fusion.8), channel_id=1, source_target_pairs={{0,1},{1,2},{2,3},{3,0},{4,5},{5,6},{6,7},{7,4},{8,9},{9,10},{10,1... | collective-permute-start | bytes 393224 | tf_op jit(solution)/shard_map/ppermute | solution.py:303
  100.2 6.4 %collective-permute-start.15 = (bf16[512,128]{1,0:T(8,128)(2,1)S(1)}, bf16[512,128]{1,0:T(8,128)(2,1)S(1)}, u32[]{:S(2)}, u32[]{:S(2)}) collective-permute-start(bf16[512,128]{1,0:T(8,128)(2,1)S(1)} %fusion.8), channel_id=1, source_target_pairs={{0,3},{1,0},{2,1},{3,2},{4,7},{5,4},{6,5},{7,6},{8,11},{9,8},{10,9... | collective-permute-start | bytes 393224 | tf_op jit(solution)/shard_map/ppermute | solution.py:303
  106.6 21.3 %collective-permute-start.16 = (f32[512,128]{1,0:T(8,128)S(1)}, f32[512,128]{1,0:T(8,128)S(1)}, u32[]{:S(2)}, u32[]{:S(2)}) collective-permute-start(f32[512,128]{1,0:T(8,128)S(1)} %add_add_fusion.1), channel_id=1, source_target_pairs={{0,8},{1,9},{2,10},{3,11},{4,12},{5,13},{6,14},{7,15},{8,0},{9,1},... | collective-permute-start | bytes 786440 | tf_op jit(solution)/shard_map/ppermute | solution.py:303
  109.7 18.2 %collective-permute-start.17 = (f32[512,128]{1,0:T(8,128)S(1)}, f32[512,128]{1,0:T(8,128)S(1)}, u32[]{:S(2)}, u32[]{:S(2)}) collective-permute-start(f32[512,128]{1,0:T(8,128)S(1)} %add_add_fusion.1), channel_id=1, source_target_pairs={{0,4},{1,5},{2,6},{3,7},{4,8},{5,9},{6,10},{7,11},{8,12},{9,13},{1... | collective-permute-start | bytes 786440 | tf_op jit(solution)/shard_map/ppermute | solution.py:303
  110.1 17.9 %collective-permute-start.18 = (f32[512,128]{1,0:T(8,128)S(1)}, f32[512,128]{1,0:T(8,128)S(1)}, u32[]{:S(2)}, u32[]{:S(2)}) collective-permute-start(f32[512,128]{1,0:T(8,128)S(1)} %add_add_fusion.1), channel_id=1, source_target_pairs={{0,12},{1,13},{2,14},{3,15},{4,0},{5,1},{6,2},{7,3},{8,4},{9,5},{1... | collective-permute-start | bytes 786440 | tf_op jit(solution)/shard_map/ppermute | solution.py:303
  142.5 6.5 %collective-permute-start.20 = (f32[32,544]{0,1:T(8,128)S(1)}, f32[32,544]{0,1:T(8,128)S(1)}, u32[]{:S(2)}, u32[]{:S(2)}) collective-permute-start(f32[32,544]{0,1:T(8,128)S(1)} %copy.46), channel_id=1, source_target_pairs={{0,96},{16,112},{32,0},{48,16},{64,32},{80,48},{96,64},{112,80},{1... | collective-permute-start | bytes 208904 | tf_op jit(solution)/shard_map/ppermute | solution.py:353
  143.1 7.0 %collective-permute-start.19 = (f32[32,544]{0,1:T(8,128)S(1)}, f32[32,544]{0,1:T(8,128)S(1)}, u32[]{:S(2)}, u32[]{:S(2)}) collective-permute-start(f32[32,544]{0,1:T(8,128)S(1)} %copy.46), channel_id=1, source_target_pairs={{0,64},{16,80},{32,96},{48,112},{64,0},{80,16},{96,32},{112,48},{1... | collective-permute-start | bytes 208904 | tf_op jit(solution)/shard_map/ppermute | solution.py:353
  145.1 13.2 %collective-permute-start.21 = (f32[32,544]{0,1:T(8,128)S(1)}, f32[32,544]{0,1:T(8,128)S(1)}, u32[]{:S(2)}, u32[]{:S(2)}) collective-permute-start(f32[32,544]{0,1:T(8,128)S(1)} %copy.46), channel_id=1, source_target_pairs={{0,32},{16,48},{32,64},{48,80},{64,96},{80,112},{96,0},{112,16},{1... | collective-permute-start | bytes 208904 | tf_op jit(solution)/shard_map/ppermute | solution.py:353
  158.6 2.6 %copy-start.4 = (f32[32,2080]{1,0:T(8,128)}, f32[32,2080]{1,0:T(8,128)S(1)}, u32[]{:S(2)}) copy-start(f32[32,2080]{1,0:T(8,128)S(1)} %constant_dynamic-update-slice_fusion.refs_0_) | copy-start | bytes 798724
  158.6 2.6 %collective-permute-start.22 = (f32[32,2080]{1,0:T(8,128)S(1)}, f32[32,2080]{1,0:T(8,128)S(1)}, u32[]{:S(2)}, u32[]{:S(2)}) collective-permute-start(f32[32,2080]{1,0:T(8,128)S(1)} %constant_dynamic-update-slice_fusion.refs_0_), channel_id=1, source_target_pairs={{0,16},{16,0},{32,48},{48,32},{64,80},{80,64},{96,112},{112,96},{1... | collective-permute-start | bytes 798728 | tf_op jit(solution)/shard_map/ppermute | solution.py:356
  161.2 0.7 copy-start.6
  170.5 6.8 %collective-permute-start.24 = (f32[32,544]{1,0:T(8,128)S(1)}, f32[32,544]{1,0:T(8,128)S(1)}, u32[]{:S(2)}, u32[]{:S(2)}) collective-permute-start(f32[32,544]{1,0:T(8,128)S(1)} %pad_maximum_fusion.1), channel_id=1, source_target_pairs={{0,96},{16,112},{32,0},{48,16},{64,32},{80,48},{96,64},{112,80},{1... | collective-permute-start | bytes 208904 | tf_op jit(solution)/shard_map/ppermute | solution.py:353
  171.1 6.2 %collective-permute-start.23 = (f32[32,544]{1,0:T(8,128)S(1)}, f32[32,544]{1,0:T(8,128)S(1)}, u32[]{:S(2)}, u32[]{:S(2)}) collective-permute-start(f32[32,544]{1,0:T(8,128)S(1)} %pad_maximum_fusion.1), channel_id=1, source_target_pairs={{0,64},{16,80},{32,96},{48,112},{64,0},{80,16},{96,32},{112,48},{1... | collective-permute-start | bytes 208904 | tf_op jit(solution)/shard_map/ppermute | solution.py:353
  172.8 5.4 %collective-permute-start.25 = (f32[32,544]{1,0:T(8,128)S(1)}, f32[32,544]{1,0:T(8,128)S(1)}, u32[]{:S(2)}, u32[]{:S(2)}) collective-permute-start(f32[32,544]{1,0:T(8,128)S(1)} %pad_maximum_fusion.1), channel_id=1, source_target_pairs={{0,32},{16,48},{32,64},{48,80},{64,96},{80,112},{96,0},{112,16},{1... | collective-permute-start | bytes 208904 | tf_op jit(solution)/shard_map/ppermute | solution.py:353
  178.2 4.7 %copy-start.3 = (f32[32,2080]{1,0:T(8,128)}, f32[32,2080]{1,0:T(8,128)S(1)}, u32[]{:S(2)}) copy-start(f32[32,2080]{1,0:T(8,128)S(1)} %get-tuple-element.22.refs_0_) | copy-start | bytes 798724
  178.2 4.7 %collective-permute-start.26 = (f32[32,2080]{1,0:T(8,128)S(1)}, f32[32,2080]{1,0:T(8,128)S(1)}, u32[]{:S(2)}, u32[]{:S(2)}) collective-permute-start(f32[32,2080]{1,0:T(8,128)S(1)} %get-tuple-element.22.refs_0_), channel_id=1, source_target_pairs={{0,16},{16,0},{32,48},{48,32},{64,80},{80,64},{96,112},{112,96},{1... | collective-permute-start | bytes 798728 | tf_op jit(solution)/shard_map/ppermute | solution.py:356
  182.9 6.5 %copy-start = (f32[32,512]{1,0:T(8,128)S(1)}, f32[32,512]{1,0:T(8,128)}, u32[]{:S(2)}) copy-start(f32[32,512]{1,0:T(8,128)} %apply.2) | copy-start | bytes 196612
  182.9 0.7 copy-start.5
  190.4 12.7 %collective-permute-start.27 = (f32[32,32]{1,0:T(8,128)S(1)}, f32[32,32]{1,0:T(8,128)S(1)}, u32[]{:S(2)}, u32[]{:S(2)}) collective-permute-start(f32[32,32]{1,0:T(8,128)S(1)} %fusion.47), channel_id=1, source_target_pairs={{0,64},{16,80},{32,96},{48,112},{64,0},{80,16},{96,32},{112,48},{1... | collective-permute-start | bytes 12296 | tf_op jit(solution)/shard_map/ppermute | solution.py:303
  192.3 10.9 %collective-permute-start.28 = (f32[32,32]{1,0:T(8,128)S(1)}, f32[32,32]{1,0:T(8,128)S(1)}, u32[]{:S(2)}, u32[]{:S(2)}) collective-permute-start(f32[32,32]{1,0:T(8,128)S(1)} %fusion.47), channel_id=1, source_target_pairs={{0,32},{16,48},{32,64},{48,80},{64,96},{80,112},{96,0},{112,16},{1... | collective-permute-start | bytes 12296 | tf_op jit(solution)/shard_map/ppermute | solution.py:303
  192.8 10.3 %collective-permute-start.29 = (f32[32,32]{1,0:T(8,128)S(1)}, f32[32,32]{1,0:T(8,128)S(1)}, u32[]{:S(2)}, u32[]{:S(2)}) collective-permute-start(f32[32,32]{1,0:T(8,128)S(1)} %fusion.47), channel_id=1, source_target_pairs={{0,96},{16,112},{32,0},{48,16},{64,32},{80,48},{96,64},{112,80},{1... | collective-permute-start | bytes 12296 | tf_op jit(solution)/shard_map/ppermute | solution.py:303
  203.2 1.8 collective-permute-start.30
where the time goes:
time: 207 us; the launch traced here: 206 us
  Pallas kernels  83.7 us (40%)
  starting transfers between devices  38.8 us (19%)
  waiting for transfers between devices  31.8 us (15%)
  local copies, waits for them, and re-layouts  24.2 us (12%)
  other arithmetic  20.3 us (10%)
  matrix products  5.96 us (3%)
    pallas_call x1, Pallas kernels, pick(): pl.pallas_call(pick_kernel, grid_spec=pltpu.PrefetchScalarGridSpec(num_sc...  42.3 us
    unnamed x27, local copies, waits for them, and re-layouts  18.7 us
    pallas_call x1, Pallas kernels, slot_map(): pl.pallas_call(slot_map_kernel, grid=(8,), in_specs=[pl.BlockSpec((64, 12...  18.3 us
    ppermute x9, starting transfers between devices, sum_four(): r1, r2, r3 = [lax.ppermute(v, axis, p) for p in perms]  15.7 us
    ppermute x6, waiting for transfers between devices, gather_all(): parts[4 - d] = lax.ppermute(v, 'row', z_send[d - 1])  12.9 us
    pallas_call x1, Pallas kernels, operator(): pl.pallas_call(operator_kernel, grid=(4,), in_specs=[pl.BlockSpec((128, 1...  11.7 us
    pallas_call x2, Pallas kernels, apply_rows(): pl.pallas_call(apply_kernel, grid=(2,), in_specs=[pl.BlockSpec((256, SNAP...  11.4 us
    ppermute x3, waiting for transfers between devices, shards(): nb_from[4 - d] = lax.ppermute(nb16, 'row', z_send[d - 1])  6.19 us
  transfers between devices with their start and end apart: 31, of which 13 were waited for; matrix products, arithmetic and copies ran while one was open for 19% of the time, Pallas kernels for 9%

commit v1 on v0

--- a/solution.py
+++ b/solution.py
@@ -206,7 +206,9 @@
         lo = jnp.broadcast_to(nb & 127, (128, 128))
         left = jnp.where(sub32 == hi, number, 0.0).astype(BF16)
         right = jnp.where(sub128 == lo, 1.0, 0.0).astype(BF16)
-        out_ref[t] = lax.dot_general(left, right, NT, preferred_element_type=F32).astype(jnp.int32)
+        r = lax.dot_general(left, right, NT, preferred_element_type=F32).astype(jnp.int32)
+        for k in range(4):
+            out_ref[pl.ds(lax.div(t, 8) * 256 + k * 64 + lax.rem(t, 8), 8, stride=8), :] = r[k * 8 : k * 8 + 8, :]
         return carry
 
     lax.fori_loop(0, 64, body, 0, unroll=8)
@@ -217,8 +219,8 @@
         slot_map_kernel,
         grid=(8,),
         in_specs=[pl.BlockSpec((64, 128), lambda i: (i, 0))],
-        out_specs=pl.BlockSpec((64, 32, 128), lambda i: (i, 0, 0)),
-        out_shape=jax.ShapeDtypeStruct((BLOCK, 32, 128), jnp.int32),
+        out_specs=pl.BlockSpec((2048, 128), lambda i: (i, 0)),
+        out_shape=jax.ShapeDtypeStruct((BLOCK * 32, 128), jnp.int32),
         cost_estimate=pl.CostEstimate(flops=1 << 20, bytes_accessed=1 << 20, transcendentals=0),
         name="slot_map",
     )(nb)
@@ -235,6 +237,20 @@
     r = lax.dot_general(parts, hi, NT, preferred_element_type=F32)
     q = lax.dot_general(parts[:64], lo, NT, preferred_element_type=F32)
     return ((r[64:] + q[32:]) + (r[32:64] + q[:32])) + r[:32]
+
+
+def store_image(image, out_ref, steps):
+    width = BLOCK // steps
+    i = pl.program_id(0)
+    out_ref[:, pl.ds(pl.multiple_of(i * width, width), width)] = image
+
+    @pl.when(i == steps - 1)
+    def _():
+        v = out_ref[:, :BLOCK]
+        rows = jnp.concatenate([v, jnp.zeros((96, BLOCK), F32)], 0)
+        out_ref[:, BLOCK:] = lax.dot_general(
+            v, rows, NT, precision=lax.Precision.HIGHEST, preferred_element_type=F32
+        )
 
 
 def operator_kernel(sum_ref, map_ref, b_ref, hi_ref, lo_ref, out_ref):
@@ -247,14 +263,16 @@
             col = slice(c * 128, (c + 1) * 128)
             values = []
             for h in range(2):
-                at = map_ref[g * 16 + h * 8 : g * 16 + h * 8 + 8, col]
+                first = (g * 2 + h) * 256 + c * 8
+                at = map_ref[first : first + 8, :]
                 value = jnp.take_along_axis(w[h], (at - 1) & 127, axis=1, mode="promise_in_bounds")
                 values.append(jnp.where(at > 0, value, 0.0))
             v = jnp.concatenate(values, 0)
             hi = v.astype(BF16)
             hi_ref[g * 16 : (g + 1) * 16, col] = hi
             lo_ref[g * 16 : (g + 1) * 16, col] = (v - hi.astype(F32)).astype(BF16)
-    out_ref[...] = times_transposed(jnp.concatenate(split3(b_ref[...]), 0), hi_ref[...], lo_ref[...])
+    image = times_transposed(jnp.concatenate(split3(b_ref[...]), 0), hi_ref[...], lo_ref[...])
+    store_image(image, out_ref, 4)
 
 
 def operator(total, slots, start):
@@ -263,18 +281,18 @@
         grid=(4,),
         in_specs=[
             pl.BlockSpec((128, 128), lambda i: (i, 0)),
-            pl.BlockSpec((128, SNAPS), lambda i: (i, 0)),
+            pl.BlockSpec((4096, 128), lambda i: (i, 0)),
             pl.BlockSpec((32, SNAPS), lambda i: (0, 0)),
         ],
         out_specs=[
             pl.BlockSpec((128, SNAPS), lambda i: (i, 0)),
             pl.BlockSpec((128, SNAPS), lambda i: (i, 0)),
-            pl.BlockSpec((32, 128), lambda i: (0, i)),
+            pl.BlockSpec((32, BLOCK + 128), lambda i: (0, 0)),
         ],
         out_shape=[
             jax.ShapeDtypeStruct((BLOCK, SNAPS), BF16),
             jax.ShapeDtypeStruct((BLOCK, SNAPS), BF16),
-            jax.ShapeDtypeStruct((32, BLOCK), F32),
+            jax.ShapeDtypeStruct((32, BLOCK + 128), F32),
         ],
         name="operator",
     )(total, slots, start)
@@ -284,7 +302,7 @@
     pieces, out_ref = refs[:-1], refs[-1]
     halves = len(pieces)
     full = jnp.concatenate([p[:, : SNAPS // halves] for p in pieces], 1)
-    out_ref[...] = times_transposed(jnp.concatenate(split3(full), 0), hi_ref[...], lo_ref[...])
+    store_image(times_transposed(jnp.concatenate(split3(full), 0), hi_ref[...], lo_ref[...]), out_ref, 2)
 
 
 def apply_rows(hi, lo, pieces):
@@ -293,8 +311,8 @@
         apply_kernel,
         grid=(2,),
         in_specs=[pl.BlockSpec((256, SNAPS), lambda i: (i, 0))] * 2 + [whole] * len(pieces),
-        out_specs=pl.BlockSpec((32, 256), lambda i: (0, i)),
-        out_shape=jax.ShapeDtypeStruct((32, BLOCK), F32),
+        out_specs=pl.BlockSpec((32, BLOCK + 128), lambda i: (0, 0)),
+        out_shape=jax.ShapeDtypeStruct((32, BLOCK + 128), F32),
         name="apply",
     )(hi, lo, *pieces)
 
@@ -354,13 +372,14 @@
         gram = (parts[0][:, BLOCK:] + parts[2][:, BLOCK:]) + (parts[1][:, BLOCK:] + parts[3][:, BLOCK:])
         near = jnp.concatenate([p[:, :BLOCK] for p in parts] + [gram], 1)
         far = lax.ppermute(near, "row", core_swap)
-        return (near, far), gram + far[:, SNAPS // 2 :]
-
-    hi, lo, image1 = operator(total, slots.reshape(BLOCK, SNAPS), start)
-    full1, gram1 = gather_all(jnp.concatenate([image1, mul(image1, image1, NT)], 1))
+        return (near, far), (gram + far[:, SNAPS // 2 :])[:, :32]
+
+    hi, lo, image1 = operator(total, slots, start)
+    full1, gram1 = gather_all(image1)
     image2 = apply_rows(hi, lo, full1)
-    full2, gram2 = gather_all(jnp.concatenate([image2, mul(image2, image2, NT)], 1))
-    image3 = apply_rows(hi, lo, full2)
+    full2, gram2 = gather_all(image2)
+    image3 = apply_rows(hi, lo, full2)[:, :BLOCK]
+    image2 = image2[:, :BLOCK]
     cross = mul(image2, image3, NT)
     cross = sum_four(cross, "row", z_send)
     cross = cross + lax.ppermute(cross, "row", core_swap)

time: 207 us -> 198 us (0.957)
  local copies, waits for them, and re-layouts: 24.2 us -> 11 us
  waiting for transfers between devices: 31.8 us -> 36.5 us
  matrix products: 5.96 us -> 3.03 us
  starting transfers between devices: 38.8 us -> 41.2 us
    unnamed x27 -> x26, local copies, waits for them, and re-layouts: 18.7 us -> 4.04 us
    ppermute x9, waiting for transfers between devices: 3.99 us -> 12.5 us  [sum_four(): r1, r2, r3 = [lax.ppermute(v, axis, p) for p in perms]]
    ppermute x2, starting transfers between devices: 2.74 us -> 7.53 us  [gather_all(): far = lax.ppermute(near, 'row', core_swap)]
    ppermute x6, waiting for transfers between devices: 12.9 us -> 8.71 us  [gather_all(): parts[4 - d] = lax.ppermute(v, 'row', z_send[d - 1])]
    ppermute x9, starting transfers between devices: 15.7 us -> 12.7 us  [sum_four(): r1, r2, r3 = [lax.ppermute(v, axis, p) for p in perms]]
    dot_general x9 -> x7, matrix products: 5.48 us -> 2.56 us  [mul(): lax.dot_general(a, b, dims, precision=lax.Precision.HIGHEST, preferred_el...]
    ppermute x3, waiting for transfers between devices: 5.99 us -> 8.36 us  [shards(): lax.ppermute(sent[d], 'row', z_send[d - 1])]
  transfers between devices with their start and end apart: 31 -> 31, of which waited for: 13 -> 15; matrix products, arithmetic and copies ran while one was open for 19% -> 12% of each run, Pallas kernels for 9% -> 9%
where the time goes in v1:
time: 198 us; the launch traced here: 197 us
  Pallas kernels  84.9 us (43%)
  starting transfers between devices  41.2 us (21%)
  waiting for transfers between devices  36.5 us (18%)
  other arithmetic  19.4 us (10%)
  local copies, waits for them, and re-layouts  11 us (6%)
  matrix products  3.03 us (2%)
    pallas_call x1, Pallas kernels, pick(): pl.pallas_call(pick_kernel, grid_spec=pltpu.PrefetchScalarGridSpec(num_sc...  42.3 us
    pallas_call x1, Pallas kernels, slot_map(): pl.pallas_call(slot_map_kernel, grid=(8,), in_specs=[pl.BlockSpec((64, 12...  18.4 us
    ppermute x9, starting transfers between devices, sum_four(): r1, r2, r3 = [lax.ppermute(v, axis, p) for p in perms]  12.7 us
    ppermute x9, waiting for transfers between devices, sum_four(): r1, r2, r3 = [lax.ppermute(v, axis, p) for p in perms]  12.5 us
    pallas_call x1, Pallas kernels, operator(): pl.pallas_call(operator_kernel, grid=(4,), in_specs=[pl.BlockSpec((128, 1...  12.3 us
    pallas_call x2, Pallas kernels, apply_rows(): pl.pallas_call(apply_kernel, grid=(2,), in_specs=[pl.BlockSpec((256, SNAP...  11.8 us
    ppermute x6, waiting for transfers between devices, gather_all(): parts[4 - d] = lax.ppermute(v, 'row', z_send[d - 1])  8.71 us
    ppermute x3, waiting for transfers between devices, shards(): lax.ppermute(sent[d], 'row', z_send[d - 1])  8.36 us
  transfers between devices with their start and end apart: 31, of which 15 were waited for; matrix products, arithmetic and copies ran while one was open for 12% of the time, Pallas kernels for 9%

profile of v1, /device:TPU:1, one launch (start us, length us, event | category | flops | bytes accessed | tf_op | source)
XLA Modules:
  0.0 197.2 jit_solution(1920603071326829647)
XLA Ops:
  0.7 2.6 %constant_dynamic-slice_fusion = (bf16[512,512]{1,0:T(8,128)(2,1)}, bf16[512,512]{1,0:T(8,128)(2,1)S(1)}, bf16[512,512]{1,0:T(8,128)(2,1)S(1)}, bf16[512,512]{1,0:T(8,128)(2,1)S(1)}) fusion(bf16[512,2048]{1,0:T(8,128)(2,1)} %param.6, s32[]{:T(128)S(6)} %select_n.146, s32[]{:T(128)S(6)} %select_n.142, s32[]{:T(128)S(6)} %select_n.140, s32[]{:T(128)S(6)} %select_n.144), kind=kLoop, calls=%fused_computation.105 | loop fusion | bytes 4194320 | tf_op jit(solution)/shard_map/dynamic_slice | solution.py:340
  3.4 2.5 %collective-permute-start.2 = (bf16[512,512]{1,0:T(8,128)(2,1)}, bf16[512,512]{1,0:T(8,128)(2,1)S(1)}, u32[]{:S(2)}, u32[]{:S(2)}) collective-permute-start(bf16[512,512]{1,0:T(8,128)(2,1)} %get-tuple-element.24), channel_id=1, source_target_pairs={{0,32},{16,48},{32,64},{48,80},{64,96},{80,112},{96,0},{112,16},{1... | collective-permute-start | bytes 1572872 | tf_op jit(solution)/shard_map/ppermute | solution.py:348
  5.8 2.1 %collective-permute-start = (bf16[512,512]{1,0:T(8,128)(2,1)S(1)}, bf16[512,512]{1,0:T(8,128)(2,1)S(1)}, u32[]{:S(2)}, u32[]{:S(2)}) collective-permute-start(bf16[512,512]{1,0:T(8,128)(2,1)S(1)} %get-tuple-element.25), channel_id=1, source_target_pairs={{0,96},{16,112},{32,0},{48,16},{64,32},{80,48},{96,64},{112,80},{1... | collective-permute-start | bytes 1572872 | tf_op jit(solution)/shard_map/ppermute | solution.py:348
  7.9 1.3 collective-permute-start.1
  9.3 1.3 fusion.49
  11.3 1.1 collective-permute-start.8
  12.4 18.4 %slot_map.1.map_ref = s32[16384,128]{1,0:T(8,128)} custom-call(s32[512,128]{1,0:T(8,128)} %get-tuple-element.32.nb_ref), custom_call_target="tpu_custom_call" | custom-call | flops 1048576 | bytes 1048576 | tf_op jit(solution)/shard_map/slot_map/pallas_call | solution.py:218
  30.9 2.7 %collective-permute-done.9 = s16[512,128]{1,0:T(8,128)(2,1)} collective-permute-done((s16[512,128]{1,0:T(8,128)(2,1)S(1)}, s16[512,128]{1,0:T(8,128)(2,1)}, u32[]{:S(2)}, u32[]{:S(2)}) %collective-permute-start.9) | collective-permute-done | bytes 131104 | tf_op jit(solution)/shard_map/ppermute | solution.py:345
  33.5 1.6 collective-permute-start.7
  35.1 0.9 bitcast_convert_fusion
  36.1 1.6 collective-permute-done.8
  37.7 1.5 collective-permute-start.3
  39.8 0.9 bitcast_convert_fusion.1
  43.0 42.3 %pick.1 = f32[8,256,128]{2,1,0:T(8,128)S(1)} custom-call(s32[2]{0:T(128)S(1)} %pad_add_fusion.1.where_ref, bf16[512,512]{1,0:T(8,128)(2,1)S(1)} %get-tuple-element.26.p0, bf16[512,512]{1,0:T(8,128)(2,1)S(1)} %collective-permute-done.p1, bf16[512,512]{1,0:T(8,128)(2,1)S(1)} %collective-permute-done.1.p2, bf16[512,512]{1,0:T(8,128)(2,1)S(1)} %collective-permute-done.2.p3, ...), custom_call_target="tpu_custom_call" | custom-call | tf_op jit(solution)/shard_map/pick/pallas_call | solution.py:169
  85.5 1.7 collective-permute-start.12
  88.0 2.3 %collective-permute-done.12 = bf16[512,128]{1,0:T(8,128)(2,1)S(1)} collective-permute-done((bf16[512,128]{1,0:T(8,128)(2,1)S(1)}, bf16[512,128]{1,0:T(8,128)(2,1)S(1)}, u32[]{:S(2)}, u32[]{:S(2)}) %collective-permute-start.12) | collective-permute-done | bytes 131104 | tf_op jit(solution)/shard_map/ppermute | solution.py:363
  90.3 2.9 %collective-permute-done.10 = bf16[512,128]{1,0:T(8,128)(2,1)S(1)} collective-permute-done((bf16[512,128]{1,0:T(8,128)(2,1)S(1)}, bf16[512,128]{1,0:T(8,128)(2,1)S(1)}, u32[]{:S(2)}, u32[]{:S(2)}) %collective-permute-start.10) | collective-permute-done | bytes 131104 | tf_op jit(solution)/shard_map/ppermute | solution.py:363
  93.2 3.1 %collective-permute-done.11 = bf16[512,128]{1,0:T(8,128)(2,1)S(1)} collective-permute-done((bf16[512,128]{1,0:T(8,128)(2,1)S(1)}, bf16[512,128]{1,0:T(8,128)(2,1)S(1)}, u32[]{:S(2)}, u32[]{:S(2)}) %collective-permute-start.11) | collective-permute-done | bytes 131104 | tf_op jit(solution)/shard_map/ppermute | solution.py:363
  96.4 2.5 %collective-permute-start.15 = (bf16[512,128]{1,0:T(8,128)(2,1)S(1)}, bf16[512,128]{1,0:T(8,128)(2,1)S(1)}, u32[]{:S(2)}, u32[]{:S(2)}) collective-permute-start(bf16[512,128]{1,0:T(8,128)(2,1)S(1)} %fusion.8), channel_id=1, source_target_pairs={{0,3},{1,0},{2,1},{3,2},{4,7},{5,4},{6,5},{7,6},{8,11},{9,8},{10,9... | collective-permute-start | bytes 393224 | tf_op jit(solution)/shard_map/ppermute | solution.py:321
  98.9 1.7 collective-permute-start.13
  101.4 4.7 %collective-permute-done.14 = bf16[512,128]{1,0:T(8,128)(2,1)S(1)} collective-permute-done((bf16[512,128]{1,0:T(8,128)(2,1)S(1)}, bf16[512,128]{1,0:T(8,128)(2,1)S(1)}, u32[]{:S(2)}, u32[]{:S(2)}) %collective-permute-start.14) | collective-permute-done | bytes 131104 | tf_op jit(solution)/shard_map/ppermute | solution.py:321
  106.2 2.8 %collective-permute-start.18 = (f32[512,128]{1,0:T(8,128)S(1)}, f32[512,128]{1,0:T(8,128)S(1)}, u32[]{:S(2)}, u32[]{:S(2)}) collective-permute-start(f32[512,128]{1,0:T(8,128)S(1)} %add_add_fusion.1), channel_id=1, source_target_pairs={{0,12},{1,13},{2,14},{3,15},{4,0},{5,1},{6,2},{7,3},{8,4},{9,5},{1... | collective-permute-start | bytes 786440 | tf_op jit(solution)/shard_map/ppermute | solution.py:321
  109.0 1.6 collective-permute-start.16
  110.6 0.9 broadcast_select_fusion.b_ref
  112.3 6.2 %collective-permute-done.17 = f32[512,128]{1,0:T(8,128)S(1)} collective-permute-done((f32[512,128]{1,0:T(8,128)S(1)}, f32[512,128]{1,0:T(8,128)S(1)}, u32[]{:S(2)}, u32[]{:S(2)}) %collective-permute-start.17) | collective-permute-done | bytes 262176 | tf_op jit(solution)/shard_map/ppermute | solution.py:321
  120.0 12.3 %operator.1 = (bf16[512,4096]{1,0:T(8,128)(2,1)}, bf16[512,4096]{1,0:T(8,128)(2,1)}, f32[32,640]{1,0:T(8,128)}) custom-call(f32[512,128]{1,0:T(8,128)} %add_add_fusion.sum_ref, s32[16384,128]{1,0:T(8,128)} %slot_map.1.map_ref, f32[32,4096]{1,0:T(8,128)} %broadcast_select_fusion.b_ref), custom_call_target="tpu_custom_call" | custom-call | tf_op jit(solution)/shard_map/operator/pallas_call | solution.py:279
  132.3 1.0 copy.49
  133.4 2.7 %collective-permute-start.20 = (f32[32,640]{0,1:T(8,128)S(1)}, f32[32,640]{0,1:T(8,128)S(1)}, u32[]{:S(2)}, u32[]{:S(2)}) collective-permute-start(f32[32,640]{0,1:T(8,128)S(1)} %copy.49), channel_id=1, source_target_pairs={{0,96},{16,112},{32,0},{48,16},{64,32},{80,48},{96,64},{112,80},{1... | collective-permute-start | bytes 245768 | tf_op jit(solution)/shard_map/ppermute | solution.py:371
  136.1 0.8 slice_dynamic-update-slice_fusion.3
  136.9 5.3 %collective-permute-done.21 = f32[32,640]{0,1:T(8,128)S(1)} collective-permute-done((f32[32,640]{0,1:T(8,128)S(1)}, f32[32,640]{0,1:T(8,128)S(1)}, u32[]{:S(2)}, u32[]{:S(2)}) %collective-permute-start.21) | collective-permute-done | bytes 81952 | tf_op jit(solution)/shard_map/ppermute | solution.py:371
  142.3 1.6 collective-permute-done.20
  144.1 1.8 collective-permute-done.19
  146.2 6.5 %collective-permute-start.22 = (f32[32,2176]{1,0:T(8,128)S(1)}, f32[32,2176]{1,0:T(8,128)S(1)}, u32[]{:S(2)}, u32[]{:S(2)}) collective-permute-start(f32[32,2176]{1,0:T(8,128)S(1)} %constant_dynamic-update-slice_fusion.refs_0_), channel_id=1, source_target_pairs={{0,16},{16,0},{32,48},{48,32},{64,80},{80,64},{96,112},{112,96},{1... | collective-permute-start | bytes 835592 | tf_op jit(solution)/shard_map/ppermute | solution.py:374
  152.7 1.2 collective-permute-done.22.refs_1_
  154.6 5.9 %apply.2 = f32[32,640]{1,0:T(8,128)} custom-call(bf16[512,4096]{1,0:T(8,128)(2,1)} %get-tuple-element.12.hi_ref, bf16[512,4096]{1,0:T(8,128)(2,1)} %get-tuple-element.13.lo_ref, f32[32,2176]{1,0:T(8,128)} %copy-done.3, f32[32,2176]{1,0:T(8,128)} %copy-done.6), custom_call_target="tpu_custom_call" | custom-call | tf_op jit(solution)/shard_map/apply/pallas_call | solution.py:310
  160.5 2.6 %collective-permute-start.24 = (f32[32,640]{1,0:T(8,128)}, f32[32,640]{1,0:T(8,128)S(1)}, u32[]{:S(2)}, u32[]{:S(2)}) collective-permute-start(f32[32,640]{1,0:T(8,128)} %apply.2), channel_id=1, source_target_pairs={{0,96},{16,112},{32,0},{48,16},{64,32},{80,48},{96,64},{112,80},{1... | collective-permute-start | bytes 245768 | tf_op jit(solution)/shard_map/ppermute | solution.py:371
  163.9 0.9 slice_dynamic-update-slice_fusion.4
  165.7 2.9 %cholesky.44 = f32[32,32]{1,0:T(8,128)S(1)} custom-call(f32[32,32]{1,0:T(8,128)S(1)} %fusion.31), custom_call_target="Cholesky" | custom-call | tf_op jit(solution)/shard_map/jit(cholesky)/cholesky | solution.py:388
  170.1 1.0 collective-permute-start.26
  171.7 2.4 %custom-call.6 = f32[1,32,32]{1,2,0:T(8,128)S(1)} custom-call(f32[1,32,32]{2,1,0:T(8,128)S(1)} %fusion.22), custom_call_target="InvertDiagBlocksLowerTriangular" | custom-call | tf_op jit(solution)/shard_map/jit(_solve_triangular)/triangular_solve | solution.py:389
  175.2 5.9 %apply.3 = f32[32,640]{1,0:T(8,128)} custom-call(bf16[512,4096]{1,0:T(8,128)(2,1)} %get-tuple-element.12.hi_ref, bf16[512,4096]{1,0:T(8,128)(2,1)} %get-tuple-element.13.lo_ref, f32[32,2176]{1,0:T(8,128)} %copy-done.4, f32[32,2176]{1,0:T(8,128)} %copy-done.5), custom_call_target="tpu_custom_call" | custom-call | tf_op jit(solution)/shard_map/apply/pallas_call | solution.py:310
  181.1 1.0 fusion.12
  182.1 1.3 collective-permute-start.29
  183.7 2.5 %collective-permute-start.27 = (f32[32,32]{1,0:T(8,128)S(1)}, f32[32,32]{1,0:T(8,128)S(1)}, u32[]{:S(2)}, u32[]{:S(2)}) collective-permute-start(f32[32,32]{1,0:T(8,128)S(1)} %fusion.12), channel_id=1, source_target_pairs={{0,64},{16,80},{32,96},{48,112},{64,0},{80,16},{96,32},{112,48},{1... | collective-permute-start | bytes 12296 | tf_op jit(solution)/shard_map/ppermute | solution.py:321
  187.2 2.9 %cholesky.55 = f32[32,32]{1,0:T(8,128)S(1)} custom-call(f32[32,32]{1,0:T(8,128)S(1)} %fusion.29), custom_call_target="Cholesky" | custom-call | tf_op jit(solution)/shard_map/jit(cholesky)/cholesky | solution.py:390
  191.5 2.4 %custom-call.7 = f32[1,32,32]{1,2,0:T(8,128)S(1)} custom-call(f32[1,32,32]{2,1,0:T(8,128)S(1)} %fusion.23), custom_call_target="InvertDiagBlocksLowerTriangular" | custom-call | tf_op jit(solution)/shard_map/jit(_solve_triangular)/triangular_solve | solution.py:391
  194.4 1.0 collective-permute-start.30
  195.3 0.8 fusion.16
  (104 shorter events, 17.7 us)
Async XLA Ops:
  0.6 8.6 %copy-start.1 = (s32[512,128]{1,0:T(8,128)S(1)}, s32[512,128]{1,0:T(8,128)}, u32[]{:S(2)}) copy-start(s32[512,128]{1,0:T(8,128)} %param.7) | copy-start | bytes 786436
  3.4 35.9 %collective-permute-start.2 = (bf16[512,512]{1,0:T(8,128)(2,1)}, bf16[512,512]{1,0:T(8,128)(2,1)S(1)}, u32[]{:S(2)}, u32[]{:S(2)}) collective-permute-start(bf16[512,512]{1,0:T(8,128)(2,1)} %get-tuple-element.24), channel_id=1, source_target_pairs={{0,32},{16,48},{32,64},{48,80},{64,96},{80,112},{96,0},{112,16},{1... | collective-permute-start | bytes 1572872 | tf_op jit(solution)/shard_map/ppermute | solution.py:348
  5.8 33.5 %collective-permute-start = (bf16[512,512]{1,0:T(8,128)(2,1)S(1)}, bf16[512,512]{1,0:T(8,128)(2,1)S(1)}, u32[]{:S(2)}, u32[]{:S(2)}) collective-permute-start(bf16[512,512]{1,0:T(8,128)(2,1)S(1)} %get-tuple-element.25), channel_id=1, source_target_pairs={{0,96},{16,112},{32,0},{48,16},{64,32},{80,48},{96,64},{112,80},{1... | collective-permute-start | bytes 1572872 | tf_op jit(solution)/shard_map/ppermute | solution.py:348
  7.9 31.8 %collective-permute-start.1 = (bf16[512,512]{1,0:T(8,128)(2,1)S(1)}, bf16[512,512]{1,0:T(8,128)(2,1)S(1)}, u32[]{:S(2)}, u32[]{:S(2)}) collective-permute-start(bf16[512,512]{1,0:T(8,128)(2,1)S(1)} %get-tuple-element.27), channel_id=1, source_target_pairs={{0,64},{16,80},{32,96},{48,112},{64,0},{80,16},{96,32},{112,48},{1... | collective-permute-start | bytes 1572872 | tf_op jit(solution)/shard_map/ppermute | solution.py:348
  10.6 23.0 %collective-permute-start.9 = (s16[512,128]{1,0:T(8,128)(2,1)S(1)}, s16[512,128]{1,0:T(8,128)(2,1)}, u32[]{:S(2)}, u32[]{:S(2)}) collective-permute-start(s16[512,128]{1,0:T(8,128)(2,1)S(1)} %get-tuple-element.31), channel_id=1, source_target_pairs={{0,32},{16,48},{32,64},{48,80},{64,96},{80,112},{96,0},{112,16},{1... | collective-permute-start | bytes 393224 | tf_op jit(solution)/shard_map/ppermute | solution.py:345
  11.3 26.4 %collective-permute-start.8 = (s16[512,128]{1,0:T(8,128)(2,1)S(1)}, s16[512,128]{1,0:T(8,128)(2,1)}, u32[]{:S(2)}, u32[]{:S(2)}) collective-permute-start(s16[512,128]{1,0:T(8,128)(2,1)S(1)} %get-tuple-element.31), channel_id=1, source_target_pairs={{0,64},{16,80},{32,96},{48,112},{64,0},{80,16},{96,32},{112,48},{1... | collective-permute-start | bytes 393224 | tf_op jit(solution)/shard_map/ppermute | solution.py:345
  33.5 7.2 %collective-permute-start.7 = (s16[512,128]{1,0:T(8,128)(2,1)S(1)}, s16[512,128]{1,0:T(8,128)(2,1)S(1)}, u32[]{:S(2)}, u32[]{:S(2)}) collective-permute-start(s16[512,128]{1,0:T(8,128)(2,1)S(1)} %get-tuple-element.31), channel_id=1, source_target_pairs={{0,96},{16,112},{32,0},{48,16},{64,32},{80,48},{96,64},{112,80},{1... | collective-permute-start | bytes 393224 | tf_op jit(solution)/shard_map/ppermute | solution.py:345
  37.7 3.8 %collective-permute-start.3 = (bf16[512,512]{1,0:T(8,128)(2,1)S(1)}, bf16[512,512]{1,0:T(8,128)(2,1)S(1)}, u32[]{:S(2)}, u32[]{:S(2)}) collective-permute-start(bf16[512,512]{1,0:T(8,128)(2,1)S(1)} %get-tuple-element.26.p0), channel_id=1, source_target_pairs={{0,16},{16,0},{32,48},{48,32},{64,80},{80,64},{96,112},{112,96},{1... | collective-permute-start | bytes 1572872 | tf_op jit(solution)/shard_map/ppermute | solution.py:349
  39.2 2.3 %collective-permute-start.6 = (bf16[512,512]{1,0:T(8,128)(2,1)S(1)}, bf16[512,512]{1,0:T(8,128)(2,1)S(1)}, u32[]{:S(2)}, u32[]{:S(2)}) collective-permute-start(bf16[512,512]{1,0:T(8,128)(2,1)S(1)} %collective-permute-done.2.p3), channel_id=1, source_target_pairs={{0,16},{16,0},{32,48},{48,32},{64,80},{80,64},{96,112},{112,96},{1... | collective-permute-start | bytes 1572872 | tf_op jit(solution)/shard_map/ppermute | solution.py:349
  39.3 3.0 %collective-permute-start.4 = (bf16[512,512]{1,0:T(8,128)(2,1)S(1)}, bf16[512,512]{1,0:T(8,128)(2,1)S(1)}, u32[]{:S(2)}, u32[]{:S(2)}) collective-permute-start(bf16[512,512]{1,0:T(8,128)(2,1)S(1)} %collective-permute-done.p1), channel_id=1, source_target_pairs={{0,16},{16,0},{32,48},{48,32},{64,80},{80,64},{96,112},{112,96},{1... | collective-permute-start | bytes 1572872 | tf_op jit(solution)/shard_map/ppermute | solution.py:349
  39.7 3.3 %collective-permute-start.5 = (bf16[512,512]{1,0:T(8,128)(2,1)S(1)}, bf16[512,512]{1,0:T(8,128)(2,1)S(1)}, u32[]{:S(2)}, u32[]{:S(2)}) collective-permute-start(bf16[512,512]{1,0:T(8,128)(2,1)S(1)} %collective-permute-done.1.p2), channel_id=1, source_target_pairs={{0,16},{16,0},{32,48},{48,32},{64,80},{80,64},{96,112},{112,96},{1... | collective-permute-start | bytes 1572872 | tf_op jit(solution)/shard_map/ppermute | solution.py:349
  43.0 57.7 %copy-start.2 = (f32[32,4096]{1,0:T(8,128)S(1)}, f32[32,4096]{1,0:T(8,128)}, u32[]{:S(2)}) copy-start(f32[32,4096]{1,0:T(8,128)} %param.8) | copy-start | bytes 1572868
  85.5 4.8 %collective-permute-start.12 = (bf16[512,128]{1,0:T(8,128)(2,1)S(1)}, bf16[512,128]{1,0:T(8,128)(2,1)S(1)}, u32[]{:S(2)}, u32[]{:S(2)}) collective-permute-start(bf16[512,128]{1,0:T(8,128)(2,1)S(1)} %bitcast.73), channel_id=1, source_target_pairs={{0,96},{16,112},{32,0},{48,16},{64,32},{80,48},{96,64},{112,80},{1... | collective-permute-start | bytes 393224 | tf_op jit(solution)/shard_map/ppermute | solution.py:363
  87.2 6.0 %collective-permute-start.10 = (bf16[512,128]{1,0:T(8,128)(2,1)S(1)}, bf16[512,128]{1,0:T(8,128)(2,1)S(1)}, u32[]{:S(2)}, u32[]{:S(2)}) collective-permute-start(bf16[512,128]{1,0:T(8,128)(2,1)S(1)} %bitcast.72), channel_id=1, source_target_pairs={{0,64},{16,80},{32,96},{48,112},{64,0},{80,16},{96,32},{112,48},{1... | collective-permute-start | bytes 393224 | tf_op jit(solution)/shard_map/ppermute | solution.py:363
  87.2 9.1 %collective-permute-start.11 = (bf16[512,128]{1,0:T(8,128)(2,1)S(1)}, bf16[512,128]{1,0:T(8,128)(2,1)S(1)}, u32[]{:S(2)}, u32[]{:S(2)}) collective-permute-start(bf16[512,128]{1,0:T(8,128)(2,1)S(1)} %bitcast.71), channel_id=1, source_target_pairs={{0,32},{16,48},{32,64},{48,80},{64,96},{80,112},{96,0},{112,16},{1... | collective-permute-start | bytes 393224 | tf_op jit(solution)/shard_map/ppermute | solution.py:363
  96.4 5.0 %collective-permute-start.15 = (bf16[512,128]{1,0:T(8,128)(2,1)S(1)}, bf16[512,128]{1,0:T(8,128)(2,1)S(1)}, u32[]{:S(2)}, u32[]{:S(2)}) collective-permute-start(bf16[512,128]{1,0:T(8,128)(2,1)S(1)} %fusion.8), channel_id=1, source_target_pairs={{0,3},{1,0},{2,1},{3,2},{4,7},{5,4},{6,5},{7,6},{8,11},{9,8},{10,9... | collective-permute-start | bytes 393224 | tf_op jit(solution)/shard_map/ppermute | solution.py:321
  98.9 7.2 %collective-permute-start.14 = (bf16[512,128]{1,0:T(8,128)(2,1)S(1)}, bf16[512,128]{1,0:T(8,128)(2,1)S(1)}, u32[]{:S(2)}, u32[]{:S(2)}) collective-permute-start(bf16[512,128]{1,0:T(8,128)(2,1)S(1)} %fusion.8), channel_id=1, source_target_pairs={{0,1},{1,2},{2,3},{3,0},{4,5},{5,6},{6,7},{7,4},{8,9},{9,10},{10,1... | collective-permute-start | bytes 393224 | tf_op jit(solution)/shard_map/ppermute | solution.py:321
  98.9 7.2 %collective-permute-start.13 = (bf16[512,128]{1,0:T(8,128)(2,1)S(1)}, bf16[512,128]{1,0:T(8,128)(2,1)S(1)}, u32[]{:S(2)}, u32[]{:S(2)}) collective-permute-start(bf16[512,128]{1,0:T(8,128)(2,1)S(1)} %fusion.8), channel_id=1, source_target_pairs={{0,2},{1,3},{2,0},{3,1},{4,6},{5,7},{6,4},{7,5},{8,10},{9,11},{10,... | collective-permute-start | bytes 393224 | tf_op jit(solution)/shard_map/ppermute | solution.py:321
  106.2 6.1 %collective-permute-start.18 = (f32[512,128]{1,0:T(8,128)S(1)}, f32[512,128]{1,0:T(8,128)S(1)}, u32[]{:S(2)}, u32[]{:S(2)}) collective-permute-start(f32[512,128]{1,0:T(8,128)S(1)} %add_add_fusion.1), channel_id=1, source_target_pairs={{0,12},{1,13},{2,14},{3,15},{4,0},{5,1},{6,2},{7,3},{8,4},{9,5},{1... | collective-permute-start | bytes 786440 | tf_op jit(solution)/shard_map/ppermute | solution.py:321
  109.0 9.5 %collective-permute-start.17 = (f32[512,128]{1,0:T(8,128)S(1)}, f32[512,128]{1,0:T(8,128)S(1)}, u32[]{:S(2)}, u32[]{:S(2)}) collective-permute-start(f32[512,128]{1,0:T(8,128)S(1)} %add_add_fusion.1), channel_id=1, source_target_pairs={{0,4},{1,5},{2,6},{3,7},{4,8},{5,9},{6,10},{7,11},{8,12},{9,13},{1... | collective-permute-start | bytes 786440 | tf_op jit(solution)/shard_map/ppermute | solution.py:321
  109.0 10.3 %collective-permute-start.16 = (f32[512,128]{1,0:T(8,128)S(1)}, f32[512,128]{1,0:T(8,128)S(1)}, u32[]{:S(2)}, u32[]{:S(2)}) collective-permute-start(f32[512,128]{1,0:T(8,128)S(1)} %add_add_fusion.1), channel_id=1, source_target_pairs={{0,8},{1,9},{2,10},{3,11},{4,12},{5,13},{6,14},{7,15},{8,0},{9,1},... | collective-permute-start | bytes 786440 | tf_op jit(solution)/shard_map/ppermute | solution.py:321
  133.3 8.9 %collective-permute-start.21 = (f32[32,640]{0,1:T(8,128)S(1)}, f32[32,640]{0,1:T(8,128)S(1)}, u32[]{:S(2)}, u32[]{:S(2)}) collective-permute-start(f32[32,640]{0,1:T(8,128)S(1)} %copy.49), channel_id=1, source_target_pairs={{0,32},{16,48},{32,64},{48,80},{64,96},{80,112},{96,0},{112,16},{1... | collective-permute-start | bytes 245768 | tf_op jit(solution)/shard_map/ppermute | solution.py:371
  133.4 10.5 %collective-permute-start.20 = (f32[32,640]{0,1:T(8,128)S(1)}, f32[32,640]{0,1:T(8,128)S(1)}, u32[]{:S(2)}, u32[]{:S(2)}) collective-permute-start(f32[32,640]{0,1:T(8,128)S(1)} %copy.49), channel_id=1, source_target_pairs={{0,96},{16,112},{32,0},{48,16},{64,32},{80,48},{96,64},{112,80},{1... | collective-permute-start | bytes 245768 | tf_op jit(solution)/shard_map/ppermute | solution.py:371
  136.1 9.8 %collective-permute-start.19 = (f32[32,640]{0,1:T(8,128)S(1)}, f32[32,640]{0,1:T(8,128)S(1)}, u32[]{:S(2)}, u32[]{:S(2)}) collective-permute-start(f32[32,640]{0,1:T(8,128)S(1)} %copy.49), channel_id=1, source_target_pairs={{0,64},{16,80},{32,96},{48,112},{64,0},{80,16},{96,32},{112,48},{1... | collective-permute-start | bytes 245768 | tf_op jit(solution)/shard_map/ppermute | solution.py:371
  146.1 7.7 %copy-start.3 = (f32[32,2176]{1,0:T(8,128)}, f32[32,2176]{1,0:T(8,128)S(1)}, u32[]{:S(2)}) copy-start(f32[32,2176]{1,0:T(8,128)S(1)} %constant_dynamic-update-slice_fusion.refs_0_) | copy-start | bytes 835588
  146.2 7.7 %collective-permute-start.22 = (f32[32,2176]{1,0:T(8,128)S(1)}, f32[32,2176]{1,0:T(8,128)S(1)}, u32[]{:S(2)}, u32[]{:S(2)}) collective-permute-start(f32[32,2176]{1,0:T(8,128)S(1)} %constant_dynamic-update-slice_fusion.refs_0_), channel_id=1, source_target_pairs={{0,16},{16,0},{32,48},{48,32},{64,80},{80,64},{96,112},{112,96},{1... | collective-permute-start | bytes 835592 | tf_op jit(solution)/shard_map/ppermute | solution.py:374
  153.9 0.7 copy-start.6
  160.5 8.8 %collective-permute-start.25 = (f32[32,640]{1,0:T(8,128)}, f32[32,640]{1,0:T(8,128)S(1)}, u32[]{:S(2)}, u32[]{:S(2)}) collective-permute-start(f32[32,640]{1,0:T(8,128)} %apply.2), channel_id=1, source_target_pairs={{0,32},{16,48},{32,64},{48,80},{64,96},{80,112},{96,0},{112,16},{1... | collective-permute-start | bytes 245768 | tf_op jit(solution)/shard_map/ppermute | solution.py:371
  160.5 8.8 %collective-permute-start.24 = (f32[32,640]{1,0:T(8,128)}, f32[32,640]{1,0:T(8,128)S(1)}, u32[]{:S(2)}, u32[]{:S(2)}) collective-permute-start(f32[32,640]{1,0:T(8,128)} %apply.2), channel_id=1, source_target_pairs={{0,96},{16,112},{32,0},{48,16},{64,32},{80,48},{96,64},{112,80},{1... | collective-permute-start | bytes 245768 | tf_op jit(solution)/shard_map/ppermute | solution.py:371
  163.2 6.1 %collective-permute-start.23 = (f32[32,640]{1,0:T(8,128)}, f32[32,640]{1,0:T(8,128)S(1)}, u32[]{:S(2)}, u32[]{:S(2)}) collective-permute-start(f32[32,640]{1,0:T(8,128)} %apply.2), channel_id=1, source_target_pairs={{0,64},{16,80},{32,96},{48,112},{64,0},{80,16},{96,32},{112,48},{1... | collective-permute-start | bytes 245768 | tf_op jit(solution)/shard_map/ppermute | solution.py:371
  170.1 4.4 %copy-start.4 = (f32[32,2176]{1,0:T(8,128)}, f32[32,2176]{1,0:T(8,128)S(1)}, u32[]{:S(2)}) copy-start(f32[32,2176]{1,0:T(8,128)S(1)} %get-tuple-element.22.refs_0_) | copy-start | bytes 835588
  170.1 4.4 %collective-permute-start.26 = (f32[32,2176]{1,0:T(8,128)S(1)}, f32[32,2176]{1,0:T(8,128)S(1)}, u32[]{:S(2)}, u32[]{:S(2)}) collective-permute-start(f32[32,2176]{1,0:T(8,128)S(1)} %get-tuple-element.22.refs_0_), channel_id=1, source_target_pairs={{0,16},{16,0},{32,48},{48,32},{64,80},{80,64},{96,112},{112,96},{1... | collective-permute-start | bytes 835592 | tf_op jit(solution)/shard_map/ppermute | solution.py:374
  174.4 6.7 %copy-start = (f32[32,640]{1,0:T(8,128)S(1)}, f32[32,640]{1,0:T(8,128)}, u32[]{:S(2)}) copy-start(f32[32,640]{1,0:T(8,128)} %apply.2) | copy-start | bytes 245764
  174.5 0.7 copy-start.5
  182.1 12.2 %collective-permute-start.29 = (f32[32,32]{1,0:T(8,128)S(1)}, f32[32,32]{1,0:T(8,128)S(1)}, u32[]{:S(2)}, u32[]{:S(2)}) collective-permute-start(f32[32,32]{1,0:T(8,128)S(1)} %fusion.12), channel_id=1, source_target_pairs={{0,96},{16,112},{32,0},{48,16},{64,32},{80,48},{96,64},{112,80},{1... | collective-permute-start | bytes 12296 | tf_op jit(solution)/shard_map/ppermute | solution.py:321
  183.4 10.9 %collective-permute-start.28 = (f32[32,32]{1,0:T(8,128)S(1)}, f32[32,32]{1,0:T(8,128)S(1)}, u32[]{:S(2)}, u32[]{:S(2)}) collective-permute-start(f32[32,32]{1,0:T(8,128)S(1)} %fusion.12), channel_id=1, source_target_pairs={{0,32},{16,48},{32,64},{48,80},{64,96},{80,112},{96,0},{112,16},{1... | collective-permute-start | bytes 12296 | tf_op jit(solution)/shard_map/ppermute | solution.py:321
  183.7 10.7 %collective-permute-start.27 = (f32[32,32]{1,0:T(8,128)S(1)}, f32[32,32]{1,0:T(8,128)S(1)}, u32[]{:S(2)}, u32[]{:S(2)}) collective-permute-start(f32[32,32]{1,0:T(8,128)S(1)} %fusion.12), channel_id=1, source_target_pairs={{0,64},{16,80},{32,96},{48,112},{64,0},{80,16},{96,32},{112,48},{1... | collective-permute-start | bytes 12296 | tf_op jit(solution)/shard_map/ppermute | solution.py:321
  194.4 1.8 collective-permute-start.30

commit v2 on v1

--- a/solution.py
+++ b/solution.py
@@ -13,7 +13,7 @@
 BLOCK = 512
 MB = 32
 PAD = SNAPS + 128
-GROUP = 8
+GROUP = 16
 NT = (((1,), (1,)), ((), ()))
 F32 = jnp.float32
 BF16 = jnp.bfloat16
@@ -363,7 +363,7 @@
     r1, r2, r3 = [lax.ppermute(sent[d], "row", z_send[d - 1]) for d in (1, 2, 3)]
     total = (chosen[0] + r2.astype(F32)) + (r1.astype(F32) + r3.astype(F32))
     total = sum_four(total.astype(BF16), "col", [col_perm(0, d) for d in (1, 2, 3)])
-    total = sum_four(total, "col", [col_perm(d, 0) for d in (1, 2, 3)])
+    total = sum_four(total.astype(BF16), "col", [col_perm(d, 0) for d in (1, 2, 3)])
 
     def gather_all(v):
         parts = [v] + [None] * 3

time: 198 us -> 193 us (0.975)
  waiting for transfers between devices: 36.5 us -> 33.7 us
    ppermute x9, waiting for transfers between devices: 12.5 us -> 8.64 us  [sum_four(): r1, r2, r3 = [lax.ppermute(v, axis, p) for p in perms]]
  transfers between devices with their start and end apart: 31 -> 31, of which waited for: 15 -> 13; matrix products, arithmetic and copies ran while one was open for 12% -> 13% of each run, Pallas kernels for 9% -> 10%
where the time goes in v2:
time: 193 us; the launch traced here: 192 us
  Pallas kernels  84 us (44%)
  starting transfers between devices  40.2 us (21%)
  waiting for transfers between devices  33.7 us (17%)
  other arithmetic  19.4 us (10%)
  local copies, waits for them, and re-layouts  11 us (6%)
  matrix products  3.03 us (2%)
    pallas_call x1, Pallas kernels, pick(): pl.pallas_call(pick_kernel, grid_spec=pltpu.PrefetchScalarGridSpec(num_sc...  41.4 us
    pallas_call x1, Pallas kernels, slot_map(): pl.pallas_call(slot_map_kernel, grid=(8,), in_specs=[pl.BlockSpec((64, 12...  18.4 us
    ppermute x9, starting transfers between devices, sum_four(): r1, r2, r3 = [lax.ppermute(v, axis, p) for p in perms]  12.7 us
    pallas_call x1, Pallas kernels, operator(): pl.pallas_call(operator_kernel, grid=(4,), in_specs=[pl.BlockSpec((128, 1...  12.3 us
    pallas_call x2, Pallas kernels, apply_rows(): pl.pallas_call(apply_kernel, grid=(2,), in_specs=[pl.BlockSpec((256, SNAP...  11.8 us
    ppermute x6, waiting for transfers between devices, gather_all(): parts[4 - d] = lax.ppermute(v, 'row', z_send[d - 1])  9.7 us
    ppermute x9, waiting for transfers between devices, sum_four(): r1, r2, r3 = [lax.ppermute(v, axis, p) for p in perms]  8.64 us
    ppermute x3, waiting for transfers between devices, shards(): lax.ppermute(sent[d], 'row', z_send[d - 1])  8.36 us
  transfers between devices with their start and end apart: 31, of which 13 were waited for; matrix products, arithmetic and copies ran while one was open for 13% of the time, Pallas kernels for 10%

profile of v2, /device:TPU:1, one launch (start us, length us, event | category | flops | bytes accessed | tf_op | source)
XLA Modules:
  0.0 192.4 jit_solution(7401987273593017662)
XLA Ops:
  0.7 2.6 %constant_dynamic-slice_fusion = (bf16[512,512]{1,0:T(8,128)(2,1)}, bf16[512,512]{1,0:T(8,128)(2,1)S(1)}, bf16[512,512]{1,0:T(8,128)(2,1)S(1)}, bf16[512,512]{1,0:T(8,128)(2,1)S(1)}) fusion(bf16[512,2048]{1,0:T(8,128)(2,1)} %param.6, s32[]{:T(128)S(6)} %select_n.146, s32[]{:T(128)S(6)} %select_n.142, s32[]{:T(128)S(6)} %select_n.140, s32[]{:T(128)S(6)} %select_n.144), kind=kLoop, calls=%fused_computation.105 | loop fusion | bytes 4194320 | tf_op jit(solution)/shard_map/dynamic_slice | solution.py:340
  3.4 2.5 %collective-permute-start.2 = (bf16[512,512]{1,0:T(8,128)(2,1)}, bf16[512,512]{1,0:T(8,128)(2,1)S(1)}, u32[]{:S(2)}, u32[]{:S(2)}) collective-permute-start(bf16[512,512]{1,0:T(8,128)(2,1)} %get-tuple-element.24), channel_id=1, source_target_pairs={{0,32},{16,48},{32,64},{48,80},{64,96},{80,112},{96,0},{112,16},{1... | collective-permute-start | bytes 1572872 | tf_op jit(solution)/shard_map/ppermute | solution.py:348
  5.8 2.1 %collective-permute-start = (bf16[512,512]{1,0:T(8,128)(2,1)S(1)}, bf16[512,512]{1,0:T(8,128)(2,1)S(1)}, u32[]{:S(2)}, u32[]{:S(2)}) collective-permute-start(bf16[512,512]{1,0:T(8,128)(2,1)S(1)} %get-tuple-element.25), channel_id=1, source_target_pairs={{0,96},{16,112},{32,0},{48,16},{64,32},{80,48},{96,64},{112,80},{1... | collective-permute-start | bytes 1572872 | tf_op jit(solution)/shard_map/ppermute | solution.py:348
  7.9 1.3 collective-permute-start.1
  9.3 1.3 fusion.49
  11.3 1.1 collective-permute-start.8
  12.4 18.4 %slot_map.1.map_ref = s32[16384,128]{1,0:T(8,128)} custom-call(s32[512,128]{1,0:T(8,128)} %get-tuple-element.32.nb_ref), custom_call_target="tpu_custom_call" | custom-call | flops 1048576 | bytes 1048576 | tf_op jit(solution)/shard_map/slot_map/pallas_call | solution.py:218
  30.9 2.7 %collective-permute-done.9 = s16[512,128]{1,0:T(8,128)(2,1)} collective-permute-done((s16[512,128]{1,0:T(8,128)(2,1)S(1)}, s16[512,128]{1,0:T(8,128)(2,1)}, u32[]{:S(2)}, u32[]{:S(2)}) %collective-permute-start.9) | collective-permute-done | bytes 131104 | tf_op jit(solution)/shard_map/ppermute | solution.py:345
  33.5 1.6 collective-permute-start.7
  35.1 0.9 bitcast_convert_fusion
  36.1 1.6 collective-permute-done.8
  37.7 1.5 collective-permute-start.3
  39.8 0.9 bitcast_convert_fusion.1
  43.0 41.4 %pick.1 = f32[8,256,128]{2,1,0:T(8,128)S(1)} custom-call(s32[2]{0:T(128)S(1)} %pad_add_fusion.1.where_ref, bf16[512,512]{1,0:T(8,128)(2,1)S(1)} %get-tuple-element.26.p0, bf16[512,512]{1,0:T(8,128)(2,1)S(1)} %collective-permute-done.p1, bf16[512,512]{1,0:T(8,128)(2,1)S(1)} %collective-permute-done.1.p2, bf16[512,512]{1,0:T(8,128)(2,1)S(1)} %collective-permute-done.2.p3, ...), custom_call_target="tpu_custom_call" | custom-call | tf_op jit(solution)/shard_map/pick/pallas_call | solution.py:169
  84.6 1.7 collective-permute-start.12
  87.1 2.3 %collective-permute-done.12 = bf16[512,128]{1,0:T(8,128)(2,1)S(1)} collective-permute-done((bf16[512,128]{1,0:T(8,128)(2,1)S(1)}, bf16[512,128]{1,0:T(8,128)(2,1)S(1)}, u32[]{:S(2)}, u32[]{:S(2)}) %collective-permute-start.12) | collective-permute-done | bytes 131104 | tf_op jit(solution)/shard_map/ppermute | solution.py:363
  89.4 2.9 %collective-permute-done.10 = bf16[512,128]{1,0:T(8,128)(2,1)S(1)} collective-permute-done((bf16[512,128]{1,0:T(8,128)(2,1)S(1)}, bf16[512,128]{1,0:T(8,128)(2,1)S(1)}, u32[]{:S(2)}, u32[]{:S(2)}) %collective-permute-start.10) | collective-permute-done | bytes 131104 | tf_op jit(solution)/shard_map/ppermute | solution.py:363
  92.3 3.1 %collective-permute-done.11 = bf16[512,128]{1,0:T(8,128)(2,1)S(1)} collective-permute-done((bf16[512,128]{1,0:T(8,128)(2,1)S(1)}, bf16[512,128]{1,0:T(8,128)(2,1)S(1)}, u32[]{:S(2)}, u32[]{:S(2)}) %collective-permute-start.11) | collective-permute-done | bytes 131104 | tf_op jit(solution)/shard_map/ppermute | solution.py:363
  95.5 2.5 %collective-permute-start.15 = (bf16[512,128]{1,0:T(8,128)(2,1)S(1)}, bf16[512,128]{1,0:T(8,128)(2,1)S(1)}, u32[]{:S(2)}, u32[]{:S(2)}) collective-permute-start(bf16[512,128]{1,0:T(8,128)(2,1)S(1)} %fusion.8), channel_id=1, source_target_pairs={{0,3},{1,0},{2,1},{3,2},{4,7},{5,4},{6,5},{7,6},{8,11},{9,8},{10,9... | collective-permute-start | bytes 393224 | tf_op jit(solution)/shard_map/ppermute | solution.py:321
  98.1 1.7 collective-permute-start.13
  100.5 4.7 %collective-permute-done.14 = bf16[512,128]{1,0:T(8,128)(2,1)S(1)} collective-permute-done((bf16[512,128]{1,0:T(8,128)(2,1)S(1)}, bf16[512,128]{1,0:T(8,128)(2,1)S(1)}, u32[]{:S(2)}, u32[]{:S(2)}) %collective-permute-start.14) | collective-permute-done | bytes 131104 | tf_op jit(solution)/shard_map/ppermute | solution.py:321
  105.3 2.8 %collective-permute-start.18 = (bf16[512,128]{1,0:T(8,128)(2,1)S(1)}, bf16[512,128]{1,0:T(8,128)(2,1)S(1)}, u32[]{:S(2)}, u32[]{:S(2)}) collective-permute-start(bf16[512,128]{1,0:T(8,128)(2,1)S(1)} %add_convert_fusion), channel_id=1, source_target_pairs={{0,12},{1,13},{2,14},{3,15},{4,0},{5,1},{6,2},{7,3},{8,4},{9,5},{1... | collective-permute-start | bytes 393224 | tf_op jit(solution)/shard_map/ppermute | solution.py:321
  108.1 1.6 collective-permute-start.16
  109.7 0.9 broadcast_select_fusion.b_ref
  110.6 3.9 %collective-permute-done.17 = bf16[512,128]{1,0:T(8,128)(2,1)S(1)} collective-permute-done((bf16[512,128]{1,0:T(8,128)(2,1)S(1)}, bf16[512,128]{1,0:T(8,128)(2,1)S(1)}, u32[]{:S(2)}, u32[]{:S(2)}) %collective-permute-start.17) | collective-permute-done | bytes 131104 | tf_op jit(solution)/shard_map/ppermute | solution.py:321
  115.3 12.3 %operator.1 = (bf16[512,4096]{1,0:T(8,128)(2,1)}, bf16[512,4096]{1,0:T(8,128)(2,1)}, f32[32,640]{1,0:T(8,128)}) custom-call(f32[512,128]{1,0:T(8,128)} %add_add_fusion.sum_ref, s32[16384,128]{1,0:T(8,128)} %slot_map.1.map_ref, f32[32,4096]{1,0:T(8,128)} %broadcast_select_fusion.b_ref), custom_call_target="tpu_custom_call" | custom-call | tf_op jit(solution)/shard_map/operator/pallas_call | solution.py:279
  127.6 1.0 copy.49
  128.7 2.7 %collective-permute-start.20 = (f32[32,640]{0,1:T(8,128)S(1)}, f32[32,640]{0,1:T(8,128)S(1)}, u32[]{:S(2)}, u32[]{:S(2)}) collective-permute-start(f32[32,640]{0,1:T(8,128)S(1)} %copy.49), channel_id=1, source_target_pairs={{0,96},{16,112},{32,0},{48,16},{64,32},{80,48},{96,64},{112,80},{1... | collective-permute-start | bytes 245768 | tf_op jit(solution)/shard_map/ppermute | solution.py:371
  131.4 0.8 slice_dynamic-update-slice_fusion.3
  132.2 4.3 %collective-permute-done.21 = f32[32,640]{0,1:T(8,128)S(1)} collective-permute-done((f32[32,640]{0,1:T(8,128)S(1)}, f32[32,640]{0,1:T(8,128)S(1)}, u32[]{:S(2)}, u32[]{:S(2)}) %collective-permute-start.21) | collective-permute-done | bytes 81952 | tf_op jit(solution)/shard_map/ppermute | solution.py:371
  136.6 1.8 collective-permute-done.20
  138.5 3.6 %collective-permute-done.19 = f32[32,640]{0,1:T(8,128)S(1)} collective-permute-done((f32[32,640]{0,1:T(8,128)S(1)}, f32[32,640]{0,1:T(8,128)S(1)}, u32[]{:S(2)}, u32[]{:S(2)}) %collective-permute-start.19) | collective-permute-done | bytes 81952 | tf_op jit(solution)/shard_map/ppermute | solution.py:371
  142.5 5.5 %collective-permute-start.22 = (f32[32,2176]{1,0:T(8,128)S(1)}, f32[32,2176]{1,0:T(8,128)S(1)}, u32[]{:S(2)}, u32[]{:S(2)}) collective-permute-start(f32[32,2176]{1,0:T(8,128)S(1)} %constant_dynamic-update-slice_fusion.refs_0_), channel_id=1, source_target_pairs={{0,16},{16,0},{32,48},{48,32},{64,80},{80,64},{96,112},{112,96},{1... | collective-permute-start | bytes 835592 | tf_op jit(solution)/shard_map/ppermute | solution.py:374
  147.9 1.2 collective-permute-done.22.refs_1_
  149.8 5.9 %apply.2 = f32[32,640]{1,0:T(8,128)} custom-call(bf16[512,4096]{1,0:T(8,128)(2,1)} %get-tuple-element.12.hi_ref, bf16[512,4096]{1,0:T(8,128)(2,1)} %get-tuple-element.13.lo_ref, f32[32,2176]{1,0:T(8,128)} %copy-done.3, f32[32,2176]{1,0:T(8,128)} %copy-done.6), custom_call_target="tpu_custom_call" | custom-call | tf_op jit(solution)/shard_map/apply/pallas_call | solution.py:310
  155.9 2.6 %collective-permute-start.24 = (f32[32,640]{1,0:T(8,128)}, f32[32,640]{1,0:T(8,128)S(1)}, u32[]{:S(2)}, u32[]{:S(2)}) collective-permute-start(f32[32,640]{1,0:T(8,128)} %apply.2), channel_id=1, source_target_pairs={{0,96},{16,112},{32,0},{48,16},{64,32},{80,48},{96,64},{112,80},{1... | collective-permute-start | bytes 245768 | tf_op jit(solution)/shard_map/ppermute | solution.py:371
  159.2 0.9 slice_dynamic-update-slice_fusion.4
  161.0 2.9 %cholesky.44 = f32[32,32]{1,0:T(8,128)S(1)} custom-call(f32[32,32]{1,0:T(8,128)S(1)} %fusion.31), custom_call_target="Cholesky" | custom-call | tf_op jit(solution)/shard_map/jit(cholesky)/cholesky | solution.py:388
  165.4 1.0 collective-permute-start.26
  167.1 2.4 %custom-call.6 = f32[1,32,32]{1,2,0:T(8,128)S(1)} custom-call(f32[1,32,32]{2,1,0:T(8,128)S(1)} %fusion.22), custom_call_target="InvertDiagBlocksLowerTriangular" | custom-call | tf_op jit(solution)/shard_map/jit(_solve_triangular)/triangular_solve | solution.py:389
  170.5 5.9 %apply.3 = f32[32,640]{1,0:T(8,128)} custom-call(bf16[512,4096]{1,0:T(8,128)(2,1)} %get-tuple-element.12.hi_ref, bf16[512,4096]{1,0:T(8,128)(2,1)} %get-tuple-element.13.lo_ref, f32[32,2176]{1,0:T(8,128)} %copy-done.4, f32[32,2176]{1,0:T(8,128)} %copy-done.5), custom_call_target="tpu_custom_call" | custom-call | tf_op jit(solution)/shard_map/apply/pallas_call | solution.py:310
  176.4 1.0 fusion.12
  177.4 1.2 collective-permute-start.29
  179.0 2.4 %collective-permute-start.27 = (f32[32,32]{1,0:T(8,128)S(1)}, f32[32,32]{1,0:T(8,128)S(1)}, u32[]{:S(2)}, u32[]{:S(2)}) collective-permute-start(f32[32,32]{1,0:T(8,128)S(1)} %fusion.12), channel_id=1, source_target_pairs={{0,64},{16,80},{32,96},{48,112},{64,0},{80,16},{96,32},{112,48},{1... | collective-permute-start | bytes 12296 | tf_op jit(solution)/shard_map/ppermute | solution.py:321
  182.5 2.9 %cholesky.55 = f32[32,32]{1,0:T(8,128)S(1)} custom-call(f32[32,32]{1,0:T(8,128)S(1)} %fusion.29), custom_call_target="Cholesky" | custom-call | tf_op jit(solution)/shard_map/jit(cholesky)/cholesky | solution.py:390
  186.8 2.4 %custom-call.7 = f32[1,32,32]{1,2,0:T(8,128)S(1)} custom-call(f32[1,32,32]{2,1,0:T(8,128)S(1)} %fusion.23), custom_call_target="InvertDiagBlocksLowerTriangular" | custom-call | tf_op jit(solution)/shard_map/jit(_solve_triangular)/triangular_solve | solution.py:391
  189.6 1.0 collective-permute-start.30
  190.6 0.8 fusion.16
  (104 shorter events, 16.3 us)
Async XLA Ops:
  0.6 8.6 %copy-start.1 = (s32[512,128]{1,0:T(8,128)S(1)}, s32[512,128]{1,0:T(8,128)}, u32[]{:S(2)}) copy-start(s32[512,128]{1,0:T(8,128)} %param.7) | copy-start | bytes 786436
  3.4 35.9 %collective-permute-start.2 = (bf16[512,512]{1,0:T(8,128)(2,1)}, bf16[512,512]{1,0:T(8,128)(2,1)S(1)}, u32[]{:S(2)}, u32[]{:S(2)}) collective-permute-start(bf16[512,512]{1,0:T(8,128)(2,1)} %get-tuple-element.24), channel_id=1, source_target_pairs={{0,32},{16,48},{32,64},{48,80},{64,96},{80,112},{96,0},{112,16},{1... | collective-permute-start | bytes 1572872 | tf_op jit(solution)/shard_map/ppermute | solution.py:348
  5.8 33.5 %collective-permute-start = (bf16[512,512]{1,0:T(8,128)(2,1)S(1)}, bf16[512,512]{1,0:T(8,128)(2,1)S(1)}, u32[]{:S(2)}, u32[]{:S(2)}) collective-permute-start(bf16[512,512]{1,0:T(8,128)(2,1)S(1)} %get-tuple-element.25), channel_id=1, source_target_pairs={{0,96},{16,112},{32,0},{48,16},{64,32},{80,48},{96,64},{112,80},{1... | collective-permute-start | bytes 1572872 | tf_op jit(solution)/shard_map/ppermute | solution.py:348
  7.9 31.8 %collective-permute-start.1 = (bf16[512,512]{1,0:T(8,128)(2,1)S(1)}, bf16[512,512]{1,0:T(8,128)(2,1)S(1)}, u32[]{:S(2)}, u32[]{:S(2)}) collective-permute-start(bf16[512,512]{1,0:T(8,128)(2,1)S(1)} %get-tuple-element.27), channel_id=1, source_target_pairs={{0,64},{16,80},{32,96},{48,112},{64,0},{80,16},{96,32},{112,48},{1... | collective-permute-start | bytes 1572872 | tf_op jit(solution)/shard_map/ppermute | solution.py:348
  10.6 23.0 %collective-permute-start.9 = (s16[512,128]{1,0:T(8,128)(2,1)S(1)}, s16[512,128]{1,0:T(8,128)(2,1)}, u32[]{:S(2)}, u32[]{:S(2)}) collective-permute-start(s16[512,128]{1,0:T(8,128)(2,1)S(1)} %get-tuple-element.31), channel_id=1, source_target_pairs={{0,32},{16,48},{32,64},{48,80},{64,96},{80,112},{96,0},{112,16},{1... | collective-permute-start | bytes 393224 | tf_op jit(solution)/shard_map/ppermute | solution.py:345
  11.3 26.4 %collective-permute-start.8 = (s16[512,128]{1,0:T(8,128)(2,1)S(1)}, s16[512,128]{1,0:T(8,128)(2,1)}, u32[]{:S(2)}, u32[]{:S(2)}) collective-permute-start(s16[512,128]{1,0:T(8,128)(2,1)S(1)} %get-tuple-element.31), channel_id=1, source_target_pairs={{0,64},{16,80},{32,96},{48,112},{64,0},{80,16},{96,32},{112,48},{1... | collective-permute-start | bytes 393224 | tf_op jit(solution)/shard_map/ppermute | solution.py:345
  33.5 7.2 %collective-permute-start.7 = (s16[512,128]{1,0:T(8,128)(2,1)S(1)}, s16[512,128]{1,0:T(8,128)(2,1)S(1)}, u32[]{:S(2)}, u32[]{:S(2)}) collective-permute-start(s16[512,128]{1,0:T(8,128)(2,1)S(1)} %get-tuple-element.31), channel_id=1, source_target_pairs={{0,96},{16,112},{32,0},{48,16},{64,32},{80,48},{96,64},{112,80},{1... | collective-permute-start | bytes 393224 | tf_op jit(solution)/shard_map/ppermute | solution.py:345
  37.7 3.8 %collective-permute-start.3 = (bf16[512,512]{1,0:T(8,128)(2,1)S(1)}, bf16[512,512]{1,0:T(8,128)(2,1)S(1)}, u32[]{:S(2)}, u32[]{:S(2)}) collective-permute-start(bf16[512,512]{1,0:T(8,128)(2,1)S(1)} %get-tuple-element.26.p0), channel_id=1, source_target_pairs={{0,16},{16,0},{32,48},{48,32},{64,80},{80,64},{96,112},{112,96},{1... | collective-permute-start | bytes 1572872 | tf_op jit(solution)/shard_map/ppermute | solution.py:349
  39.2 2.3 %collective-permute-start.6 = (bf16[512,512]{1,0:T(8,128)(2,1)S(1)}, bf16[512,512]{1,0:T(8,128)(2,1)S(1)}, u32[]{:S(2)}, u32[]{:S(2)}) collective-permute-start(bf16[512,512]{1,0:T(8,128)(2,1)S(1)} %collective-permute-done.2.p3), channel_id=1, source_target_pairs={{0,16},{16,0},{32,48},{48,32},{64,80},{80,64},{96,112},{112,96},{1... | collective-permute-start | bytes 1572872 | tf_op jit(solution)/shard_map/ppermute | solution.py:349
  39.3 3.0 %collective-permute-start.4 = (bf16[512,512]{1,0:T(8,128)(2,1)S(1)}, bf16[512,512]{1,0:T(8,128)(2,1)S(1)}, u32[]{:S(2)}, u32[]{:S(2)}) collective-permute-start(bf16[512,512]{1,0:T(8,128)(2,1)S(1)} %collective-permute-done.p1), channel_id=1, source_target_pairs={{0,16},{16,0},{32,48},{48,32},{64,80},{80,64},{96,112},{112,96},{1... | collective-permute-start | bytes 1572872 | tf_op jit(solution)/shard_map/ppermute | solution.py:349
  39.7 3.3 %collective-permute-start.5 = (bf16[512,512]{1,0:T(8,128)(2,1)S(1)}, bf16[512,512]{1,0:T(8,128)(2,1)S(1)}, u32[]{:S(2)}, u32[]{:S(2)}) collective-permute-start(bf16[512,512]{1,0:T(8,128)(2,1)S(1)} %collective-permute-done.1.p2), channel_id=1, source_target_pairs={{0,16},{16,0},{32,48},{48,32},{64,80},{80,64},{96,112},{112,96},{1... | collective-permute-start | bytes 1572872 | tf_op jit(solution)/shard_map/ppermute | solution.py:349
  43.0 56.8 %copy-start.2 = (f32[32,4096]{1,0:T(8,128)S(1)}, f32[32,4096]{1,0:T(8,128)}, u32[]{:S(2)}) copy-start(f32[32,4096]{1,0:T(8,128)} %param.8) | copy-start | bytes 1572868
  84.6 4.8 %collective-permute-start.12 = (bf16[512,128]{1,0:T(8,128)(2,1)S(1)}, bf16[512,128]{1,0:T(8,128)(2,1)S(1)}, u32[]{:S(2)}, u32[]{:S(2)}) collective-permute-start(bf16[512,128]{1,0:T(8,128)(2,1)S(1)} %bitcast.73), channel_id=1, source_target_pairs={{0,96},{16,112},{32,0},{48,16},{64,32},{80,48},{96,64},{112,80},{1... | collective-permute-start | bytes 393224 | tf_op jit(solution)/shard_map/ppermute | solution.py:363
  86.3 6.0 %collective-permute-start.10 = (bf16[512,128]{1,0:T(8,128)(2,1)S(1)}, bf16[512,128]{1,0:T(8,128)(2,1)S(1)}, u32[]{:S(2)}, u32[]{:S(2)}) collective-permute-start(bf16[512,128]{1,0:T(8,128)(2,1)S(1)} %bitcast.72), channel_id=1, source_target_pairs={{0,64},{16,80},{32,96},{48,112},{64,0},{80,16},{96,32},{112,48},{1... | collective-permute-start | bytes 393224 | tf_op jit(solution)/shard_map/ppermute | solution.py:363
  86.3 9.1 %collective-permute-start.11 = (bf16[512,128]{1,0:T(8,128)(2,1)S(1)}, bf16[512,128]{1,0:T(8,128)(2,1)S(1)}, u32[]{:S(2)}, u32[]{:S(2)}) collective-permute-start(bf16[512,128]{1,0:T(8,128)(2,1)S(1)} %bitcast.71), channel_id=1, source_target_pairs={{0,32},{16,48},{32,64},{48,80},{64,96},{80,112},{96,0},{112,16},{1... | collective-permute-start | bytes 393224 | tf_op jit(solution)/shard_map/ppermute | solution.py:363
  95.5 5.0 %collective-permute-start.15 = (bf16[512,128]{1,0:T(8,128)(2,1)S(1)}, bf16[512,128]{1,0:T(8,128)(2,1)S(1)}, u32[]{:S(2)}, u32[]{:S(2)}) collective-permute-start(bf16[512,128]{1,0:T(8,128)(2,1)S(1)} %fusion.8), channel_id=1, source_target_pairs={{0,3},{1,0},{2,1},{3,2},{4,7},{5,4},{6,5},{7,6},{8,11},{9,8},{10,9... | collective-permute-start | bytes 393224 | tf_op jit(solution)/shard_map/ppermute | solution.py:321
  98.0 7.2 %collective-permute-start.14 = (bf16[512,128]{1,0:T(8,128)(2,1)S(1)}, bf16[512,128]{1,0:T(8,128)(2,1)S(1)}, u32[]{:S(2)}, u32[]{:S(2)}) collective-permute-start(bf16[512,128]{1,0:T(8,128)(2,1)S(1)} %fusion.8), channel_id=1, source_target_pairs={{0,1},{1,2},{2,3},{3,0},{4,5},{5,6},{6,7},{7,4},{8,9},{9,10},{10,1... | collective-permute-start | bytes 393224 | tf_op jit(solution)/shard_map/ppermute | solution.py:321
  98.1 7.2 %collective-permute-start.13 = (bf16[512,128]{1,0:T(8,128)(2,1)S(1)}, bf16[512,128]{1,0:T(8,128)(2,1)S(1)}, u32[]{:S(2)}, u32[]{:S(2)}) collective-permute-start(bf16[512,128]{1,0:T(8,128)(2,1)S(1)} %fusion.8), channel_id=1, source_target_pairs={{0,2},{1,3},{2,0},{3,1},{4,6},{5,7},{6,4},{7,5},{8,10},{9,11},{10,... | collective-permute-start | bytes 393224 | tf_op jit(solution)/shard_map/ppermute | solution.py:321
  105.3 5.3 %collective-permute-start.18 = (bf16[512,128]{1,0:T(8,128)(2,1)S(1)}, bf16[512,128]{1,0:T(8,128)(2,1)S(1)}, u32[]{:S(2)}, u32[]{:S(2)}) collective-permute-start(bf16[512,128]{1,0:T(8,128)(2,1)S(1)} %add_convert_fusion), channel_id=1, source_target_pairs={{0,12},{1,13},{2,14},{3,15},{4,0},{5,1},{6,2},{7,3},{8,4},{9,5},{1... | collective-permute-start | bytes 393224 | tf_op jit(solution)/shard_map/ppermute | solution.py:321
  108.1 6.4 %collective-permute-start.17 = (bf16[512,128]{1,0:T(8,128)(2,1)S(1)}, bf16[512,128]{1,0:T(8,128)(2,1)S(1)}, u32[]{:S(2)}, u32[]{:S(2)}) collective-permute-start(bf16[512,128]{1,0:T(8,128)(2,1)S(1)} %add_convert_fusion), channel_id=1, source_target_pairs={{0,4},{1,5},{2,6},{3,7},{4,8},{5,9},{6,10},{7,11},{8,12},{9,13},{1... | collective-permute-start | bytes 393224 | tf_op jit(solution)/shard_map/ppermute | solution.py:321
  108.1 6.4 %collective-permute-start.16 = (bf16[512,128]{1,0:T(8,128)(2,1)S(1)}, bf16[512,128]{1,0:T(8,128)(2,1)S(1)}, u32[]{:S(2)}, u32[]{:S(2)}) collective-permute-start(bf16[512,128]{1,0:T(8,128)(2,1)S(1)} %add_convert_fusion), channel_id=1, source_target_pairs={{0,8},{1,9},{2,10},{3,11},{4,12},{5,13},{6,14},{7,15},{8,0},{9,1},... | collective-permute-start | bytes 393224 | tf_op jit(solution)/shard_map/ppermute | solution.py:321
  128.6 7.9 %collective-permute-start.21 = (f32[32,640]{0,1:T(8,128)S(1)}, f32[32,640]{0,1:T(8,128)S(1)}, u32[]{:S(2)}, u32[]{:S(2)}) collective-permute-start(f32[32,640]{0,1:T(8,128)S(1)} %copy.49), channel_id=1, source_target_pairs={{0,32},{16,48},{32,64},{48,80},{64,96},{80,112},{96,0},{112,16},{1... | collective-permute-start | bytes 245768 | tf_op jit(solution)/shard_map/ppermute | solution.py:371
  128.7 9.7 %collective-permute-start.20 = (f32[32,640]{0,1:T(8,128)S(1)}, f32[32,640]{0,1:T(8,128)S(1)}, u32[]{:S(2)}, u32[]{:S(2)}) collective-permute-start(f32[32,640]{0,1:T(8,128)S(1)} %copy.49), channel_id=1, source_target_pairs={{0,96},{16,112},{32,0},{48,16},{64,32},{80,48},{96,64},{112,80},{1... | collective-permute-start | bytes 245768 | tf_op jit(solution)/shard_map/ppermute | solution.py:371
  131.4 10.8 %collective-permute-start.19 = (f32[32,640]{0,1:T(8,128)S(1)}, f32[32,640]{0,1:T(8,128)S(1)}, u32[]{:S(2)}, u32[]{:S(2)}) collective-permute-start(f32[32,640]{0,1:T(8,128)S(1)} %copy.49), channel_id=1, source_target_pairs={{0,64},{16,80},{32,96},{48,112},{64,0},{80,16},{96,32},{112,48},{1... | collective-permute-start | bytes 245768 | tf_op jit(solution)/shard_map/ppermute | solution.py:371
  142.4 6.7 %copy-start.3 = (f32[32,2176]{1,0:T(8,128)}, f32[32,2176]{1,0:T(8,128)S(1)}, u32[]{:S(2)}) copy-start(f32[32,2176]{1,0:T(8,128)S(1)} %constant_dynamic-update-slice_fusion.refs_0_) | copy-start | bytes 835588
  142.5 6.7 %collective-permute-start.22 = (f32[32,2176]{1,0:T(8,128)S(1)}, f32[32,2176]{1,0:T(8,128)S(1)}, u32[]{:S(2)}, u32[]{:S(2)}) collective-permute-start(f32[32,2176]{1,0:T(8,128)S(1)} %constant_dynamic-update-slice_fusion.refs_0_), channel_id=1, source_target_pairs={{0,16},{16,0},{32,48},{48,32},{64,80},{80,64},{96,112},{112,96},{1... | collective-permute-start | bytes 835592 | tf_op jit(solution)/shard_map/ppermute | solution.py:374
  149.1 0.7 copy-start.6
  155.7 8.9 %collective-permute-start.25 = (f32[32,640]{1,0:T(8,128)}, f32[32,640]{1,0:T(8,128)S(1)}, u32[]{:S(2)}, u32[]{:S(2)}) collective-permute-start(f32[32,640]{1,0:T(8,128)} %apply.2), channel_id=1, source_target_pairs={{0,32},{16,48},{32,64},{48,80},{64,96},{80,112},{96,0},{112,16},{1... | collective-permute-start | bytes 245768 | tf_op jit(solution)/shard_map/ppermute | solution.py:371
  155.9 8.7 %collective-permute-start.24 = (f32[32,640]{1,0:T(8,128)}, f32[32,640]{1,0:T(8,128)S(1)}, u32[]{:S(2)}, u32[]{:S(2)}) collective-permute-start(f32[32,640]{1,0:T(8,128)} %apply.2), channel_id=1, source_target_pairs={{0,96},{16,112},{32,0},{48,16},{64,32},{80,48},{96,64},{112,80},{1... | collective-permute-start | bytes 245768 | tf_op jit(solution)/shard_map/ppermute | solution.py:371
  158.4 6.2 %collective-permute-start.23 = (f32[32,640]{1,0:T(8,128)}, f32[32,640]{1,0:T(8,128)S(1)}, u32[]{:S(2)}, u32[]{:S(2)}) collective-permute-start(f32[32,640]{1,0:T(8,128)} %apply.2), channel_id=1, source_target_pairs={{0,64},{16,80},{32,96},{48,112},{64,0},{80,16},{96,32},{112,48},{1... | collective-permute-start | bytes 245768 | tf_op jit(solution)/shard_map/ppermute | solution.py:371
  165.4 4.4 %copy-start.4 = (f32[32,2176]{1,0:T(8,128)}, f32[32,2176]{1,0:T(8,128)S(1)}, u32[]{:S(2)}) copy-start(f32[32,2176]{1,0:T(8,128)S(1)} %get-tuple-element.22.refs_0_) | copy-start | bytes 835588
  165.4 4.4 %collective-permute-start.26 = (f32[32,2176]{1,0:T(8,128)S(1)}, f32[32,2176]{1,0:T(8,128)S(1)}, u32[]{:S(2)}, u32[]{:S(2)}) collective-permute-start(f32[32,2176]{1,0:T(8,128)S(1)} %get-tuple-element.22.refs_0_), channel_id=1, source_target_pairs={{0,16},{16,0},{32,48},{48,32},{64,80},{80,64},{96,112},{112,96},{1... | collective-permute-start | bytes 835592 | tf_op jit(solution)/shard_map/ppermute | solution.py:374
  169.7 6.7 %copy-start = (f32[32,640]{1,0:T(8,128)S(1)}, f32[32,640]{1,0:T(8,128)}, u32[]{:S(2)}) copy-start(f32[32,640]{1,0:T(8,128)} %apply.2) | copy-start | bytes 245764
  169.8 0.7 copy-start.5
  177.4 12.2 %collective-permute-start.29 = (f32[32,32]{1,0:T(8,128)S(1)}, f32[32,32]{1,0:T(8,128)S(1)}, u32[]{:S(2)}, u32[]{:S(2)}) collective-permute-start(f32[32,32]{1,0:T(8,128)S(1)} %fusion.12), channel_id=1, source_target_pairs={{0,96},{16,112},{32,0},{48,16},{64,32},{80,48},{96,64},{112,80},{1... | collective-permute-start | bytes 12296 | tf_op jit(solution)/shard_map/ppermute | solution.py:321
  178.6 11.0 %collective-permute-start.28 = (f32[32,32]{1,0:T(8,128)S(1)}, f32[32,32]{1,0:T(8,128)S(1)}, u32[]{:S(2)}, u32[]{:S(2)}) collective-permute-start(f32[32,32]{1,0:T(8,128)S(1)} %fusion.12), channel_id=1, source_target_pairs={{0,32},{16,48},{32,64},{48,80},{64,96},{80,112},{96,0},{112,16},{1... | collective-permute-start | bytes 12296 | tf_op jit(solution)/shard_map/ppermute | solution.py:321
  179.0 10.6 %collective-permute-start.27 = (f32[32,32]{1,0:T(8,128)S(1)}, f32[32,32]{1,0:T(8,128)S(1)}, u32[]{:S(2)}, u32[]{:S(2)}) collective-permute-start(f32[32,32]{1,0:T(8,128)S(1)} %fusion.12), channel_id=1, source_target_pairs={{0,64},{16,80},{32,96},{48,112},{64,0},{80,16},{96,32},{112,48},{1... | collective-permute-start | bytes 12296 | tf_op jit(solution)/shard_map/ppermute | solution.py:321
  189.6 1.8 collective-permute-start.30
